TPU v7x, 32 devices: a whole 2x2x4 slice. The times are simulated.
32 devices in a mesh: slab: 8 (over z, y), grp: 4 (over x, core).
Axes of the slice: x: 2, y: 2, z: 4, core: 2. Of those that a mesh axis runs over, the one named last changes fastest.
Arguments:
- u_now: float32 [3, 128, 32, 128], P(None, 'slab', 'grp'), may hold values from -6 to 6
- u_prev: float32 [3, 128, 32, 128], P(None, 'slab', 'grp'), may hold values from -6 to 6
- force: float32 [3, 128, 32, 128], P(None, 'slab', 'grp'), may hold values from -6 to 6
- stiffness: float32 [128, 32, 128], P('slab', 'grp'), may hold values from 0.5 to 2
- broken: int32 [32, 8, 32], P('slab', 'grp'), may hold values 0 or 1
- flags: int32 [32, 8, 32], P('slab', 'grp'), may hold values 0 or 1
Outputs:
- displacement: float32 [3, 128, 32, 128], P(None, 'slab', 'grp')
- coeffs: float32 [6, 32, 128, 128], P(None, 'grp', 'slab')
All inputs are finite; a program needn't handle non-finite values. No bound on the sum of `broken` or of `flags` on one device may be relied on, other than what follows from the above.
Results may differ from a plain program's by a relative error of at most 0.0001.
Values sent between devices are 32-bit elements; how exact they have to be, the bound alone decides.
A program may use at most 64 MiB of HBM per device.

v0:
```python
import jax
import jax.numpy as jnp
import numpy as np
from jax import lax
from jax.sharding import PartitionSpec as P

STEPS = 2
ITERS = 2
LEVELS = 3


SPRING_NORMAL = 1.0
SPRING_SHEAR = 0.4
MASS_TERM = 1.0
CRACK_CUT = 0.9


def with_halo(block, sides, width):
    for axis, dim in sides:
        count = lax.axis_size(axis)
        forward = [(i, i + 1) for i in range(count - 1)]
        backward = [(target, source) for source, target in forward]
        low = lax.ppermute(
            lax.slice_in_dim(block, block.shape[dim] - width, None, axis=dim), axis, forward
        )
        high = lax.ppermute(lax.slice_in_dim(block, 0, width, axis=dim), axis, backward)
        block = jnp.concatenate([low, block, high], axis=dim)
    return block


def cosine_table():
    freq = np.arange(4)[:, None]
    place = np.arange(4)[None, :]
    factor = np.where(freq == 0, 0.5, np.sqrt(0.5))
    return factor * np.cos(np.pi * (2 * place + 1) * freq / 8.0)


def block_table(count):
    return jnp.asarray(np.kron(np.eye(count // 4), cosine_table()), jnp.float32)


def spread(mask):
    values = mask.astype(jnp.float32)
    size_a, size_b, size_c = values.shape
    wide = jnp.broadcast_to(values[:, None, :, None, :, None], (size_a, 4, size_b, 4, size_c, 4))
    return wide.reshape(size_a * 4, size_b * 4, size_c * 4)


def sides(padded, axis_index):
    leading = padded.ndim - 3

    def cut(offset):
        index_list = [slice(None)] * leading + [slice(1, -1)] * 3
        length = padded.shape[leading + axis_index]
        index_list[leading + axis_index] = slice(1 + offset, length - 1 + offset)
        return padded[tuple(index_list)]

    return (cut(1), cut(-1))


def springs(field, weight, field_pad, weight_pad):
    result = MASS_TERM * field
    for axis_index in range(3):
        upper_v, lower_v = sides(field_pad, axis_index)
        upper_w, lower_w = sides(weight_pad, axis_index)
        k_upper = 0.5 * (weight + upper_w)
        k_lower = 0.5 * (weight + lower_w)
        change = k_upper * (field - upper_v) + k_lower * (field - lower_v)
        coupling = jnp.array(
            [SPRING_NORMAL if comp == axis_index else SPRING_SHEAR for comp in range(3)],
            jnp.float32,
        ).reshape(3, 1, 1, 1)
        result = result + coupling * change
    return result


def faces(field):
    padded = with_halo(field, (("slab", 1), ("grp", 2)), 1)
    return jnp.pad(padded, ((0, 0), (0, 0), (0, 0), (1, 1)))


def stresses(carry, field_pad):
    rows_out = []
    for axis_index in range(3):
        upper_v, lower_v = sides(field_pad, axis_index)
        rows_out.append(SPRING_NORMAL * carry * 0.5 * (upper_v[axis_index] - lower_v[axis_index]))
    return jnp.stack(rows_out)


def paired_sum(residual, image):
    return lax.psum((jnp.sum(residual * residual), jnp.sum(residual * image)), ("slab", "grp"))


def lift(signal):
    even = signal[..., 0::2]
    odd = signal[..., 1::2]
    detail = odd - 0.5 * (even + jnp.roll(even, -1, axis=-1))
    approx = even + 0.25 * (jnp.roll(detail, 1, axis=-1) + detail)
    return (approx, detail)


def wavelet(signal):
    pieces = []
    approx = signal
    for level_index in range(LEVELS):
        approx, detail = lift(approx)
        pieces.insert(0, detail)
    return jnp.concatenate([approx] + pieces, axis=-1)


def body(u_now, u_prev, force, stiffness, broken, flags):
    weight = stiffness * (1.0 - CRACK_CUT * spread(broken))
    carry = spread(flags) * weight
    weight_pad = with_halo(weight, (("slab", 0), ("grp", 1)), 1)
    weight_pad = jnp.pad(weight_pad, ((0, 0), (0, 0), (1, 1)))

    def operate(field):
        return springs(field, weight, faces(field), weight_pad)

    for step_index in range(STEPS):
        rhs = MASS_TERM * (2.0 * u_now - u_prev) + force
        guess = u_now
        residual = rhs - operate(guess)
        image = operate(residual)
        norm_now, product = paired_sum(residual, image)
        alpha = norm_now / product
        direction, along = (residual, image)
        for turn_index in range(ITERS):
            guess = guess + alpha * direction
            residual = residual - alpha * along
            if turn_index + 1 < ITERS:
                image = operate(residual)
                norm_next, product = paired_sum(residual, image)
                ratio = norm_next / norm_now
                alpha = norm_next / (product - ratio * norm_next / alpha)
                direction = residual + ratio * direction
                along = image + ratio * along
                norm_now = norm_next
        u_prev = u_now
        u_now = guess
    stress = stresses(carry, faces(u_now))
    fields = jnp.concatenate([u_now, stress], axis=0)
    table_x = block_table(fields.shape[1])
    table_y = block_table(fields.shape[2])
    table_z = block_table(fields.shape[3])
    blockc = jnp.einsum("ax,hxyz->hayz", table_x, fields, precision=lax.Precision.HIGHEST)
    blockc = jnp.einsum("by,hxyz->hxbz", table_y, blockc, precision=lax.Precision.HIGHEST)
    blockc = jnp.einsum("hxyz,cz->hxyc", blockc, table_z, precision=lax.Precision.HIGHEST)
    moved = jnp.transpose(blockc, (0, 2, 3, 1))
    shipped = lax.all_to_all(moved, "slab", split_axis=2, concat_axis=3, tiled=True)
    coeffs = wavelet(shipped)
    return (u_now, coeffs)


def solution(mesh):
    return jax.shard_map(
        body,
        mesh=mesh,
        in_specs=(
            P(None, "slab", "grp", None),
            P(None, "slab", "grp", None),
            P(None, "slab", "grp", None),
            P("slab", "grp", None),
            P("slab", "grp", None),
            P("slab", "grp", None),
        ),
        out_specs=(P(None, "slab", "grp", None), P(None, "grp", "slab", None)),
        check_vma=False,
    )
```

profile of v0, /device:TPU:0, one launch (start us, length us, event | category | flops | bytes accessed | tf_op | source)
XLA Modules:
  0.0 373.0 jit_solution(14565267539432466545)
XLA Ops:
  1.8 1.6 sub.172
  3.5 4.9 %collective-permute-start.2 = (f32[1,8,128]{2,0,1:T(1,128)S(1)}, f32[1,8,128]{2,0,1:T(1,128)S(1)}, u32[]{:S(2)}, u32[]{:S(2)}) collective-permute-start(f32[1,8,128]{2,0,1:T(1,128)S(1)} %get-tuple-element.65), channel_id=1, source_target_pairs={{0,4},{4,8},{8,12},{12,16},{16,20},{20,24},{24,28},{1,5},{5,9},{9,... | collective-permute-start | bytes 12296 | tf_op jit(solution)/shard_map/ppermute | solution.py:23
  11.0 5.2 %collective-permute-start.3 = (f32[3,1,8,128]{3,1,2,0:T(1,128)S(1)}, f32[3,1,8,128]{3,1,2,0:T(1,128)S(1)}, u32[]{:S(2)}, u32[]{:S(2)}) collective-permute-start(f32[3,1,8,128]{3,1,2,0:T(1,128)S(1)} %bitcast.70), channel_id=1, source_target_pairs={{0,4},{4,8},{8,12},{12,16},{16,20},{20,24},{24,28},{1,5},{5,9},{9,... | collective-permute-start | bytes 36872 | tf_op jit(solution)/shard_map/ppermute | solution.py:23
  18.9 4.8 %collective-permute-start.7 = (f32[3,18,1,128]{3,1,2,0:T(8,128)S(1)}, f32[3,18,1,128]{3,1,2,0:T(8,128)S(1)}, u32[]{:S(2)}, u32[]{:S(2)}) collective-permute-start(f32[3,18,1,128]{3,1,2,0:T(8,128)S(1)} %get-tuple-element.40), channel_id=1, source_target_pairs={{0,1},{1,2},{2,3},{4,5},{5,6},{6,7},{8,9},{9,10},{10,11},{12,13},{... | collective-permute-start | bytes 82952 | tf_op jit(solution)/shard_map/ppermute | solution.py:23
  25.3 2.7 collective-permute-done.5
  28.8 4.8 %collective-permute-start.9 = (f32[3,1,8,128]{3,1,2,0:T(1,128)S(1)}, f32[3,1,8,128]{3,1,2,0:T(1,128)S(1)}, u32[]{:S(2)}, u32[]{:S(2)}) collective-permute-start(f32[3,1,8,128]{3,1,2,0:T(1,128)S(1)} %get-tuple-element.52), channel_id=1, source_target_pairs={{0,4},{4,8},{8,12},{12,16},{16,20},{20,24},{24,28},{1,5},{5,9},{9,... | collective-permute-start | bytes 36872 | tf_op jit(solution)/shard_map/ppermute | solution.py:23
  35.0 4.2 %collective-permute-done.8 = f32[3,1,8,128]{3,1,2,0:T(1,128)S(1)} collective-permute-done((f32[3,1,8,128]{3,1,2,0:T(1,128)S(1)}, f32[3,1,8,128]{3,1,2,0:T(1,128)S(1)}, u32[]{:S(2)}, u32[]{:S(2)}) %collective-permute-start.8) | collective-permute-done | bytes 12320 | tf_op jit(solution)/shard_map/ppermute | solution.py:26
  39.2 3.1 collective-permute-start.11
  42.4 1.3 collective-permute-start.10
  43.7 2.7 collective-permute-done.10
  47.7 42.7 %all-reduce.11 = (f32[]{:T(128)}, f32[]{:T(128)}) all-reduce(f32[]{:T(128)} %get-tuple-element.9, f32[]{:T(128)} %get-tuple-element.8), channel_id=1, replica_groups=mesh['slab'=8,'grp'=4] {'slab','grp'}, use_global_device_ids=true, to_apply=%region_1.2 | all-reduce | flops 2 | bytes 16 | tf_op jit(solution)/shard_map/psum | solution.py:91
  92.4 4.4 %collective-permute-start.13 = (f32[3,1,8,128]{3,1,2,0:T(1,128)S(1)}, f32[3,1,8,128]{3,1,2,0:T(1,128)S(1)}, u32[]{:S(2)}, u32[]{:S(2)}) collective-permute-start(f32[3,1,8,128]{3,1,2,0:T(1,128)S(1)} %get-tuple-element.50), channel_id=1, source_target_pairs={{0,4},{4,8},{8,12},{12,16},{16,20},{20,24},{24,28},{1,5},{5,9},{9,... | collective-permute-start | bytes 36872 | tf_op jit(solution)/shard_map/ppermute | solution.py:23
  98.2 4.2 %collective-permute-done.12 = f32[3,1,8,128]{3,1,2,0:T(1,128)S(1)} collective-permute-done((f32[3,1,8,128]{3,1,2,0:T(1,128)S(1)}, f32[3,1,8,128]{3,1,2,0:T(1,128)S(1)}, u32[]{:S(2)}, u32[]{:S(2)}) %collective-permute-start.12) | collective-permute-done | bytes 12320 | tf_op jit(solution)/shard_map/ppermute | solution.py:26
  102.4 1.3 collective-permute-start.15
  103.7 1.3 collective-permute-start.14
  105.0 2.1 collective-permute-done.14
  108.3 42.7 %all-reduce.10 = (f32[]{:T(128)}, f32[]{:T(128)}) all-reduce(f32[]{:T(128)} %get-tuple-element.21, f32[]{:T(128)} %fusion.87), channel_id=1, replica_groups=mesh['slab'=8,'grp'=4] {'slab','grp'}, use_global_device_ids=true, to_apply=%region_5.6 | all-reduce | flops 2 | bytes 16 | tf_op jit(solution)/shard_map/psum | solution.py:91
  155.7 4.4 %collective-permute-start.17 = (f32[3,1,8,128]{3,1,2,0:T(1,128)S(1)}, f32[3,1,8,128]{3,1,2,0:T(1,128)S(1)}, u32[]{:S(2)}, u32[]{:S(2)}) collective-permute-start(f32[3,1,8,128]{3,1,2,0:T(1,128)S(1)} %get-tuple-element.48), channel_id=1, source_target_pairs={{0,4},{4,8},{8,12},{12,16},{16,20},{20,24},{24,28},{1,5},{5,9},{9,... | collective-permute-start | bytes 36872 | tf_op jit(solution)/shard_map/ppermute | solution.py:23
  161.5 4.2 %collective-permute-done.16 = f32[3,1,8,128]{3,1,2,0:T(1,128)S(1)} collective-permute-done((f32[3,1,8,128]{3,1,2,0:T(1,128)S(1)}, f32[3,1,8,128]{3,1,2,0:T(1,128)S(1)}, u32[]{:S(2)}, u32[]{:S(2)}) %collective-permute-start.16) | collective-permute-done | bytes 12320 | tf_op jit(solution)/shard_map/ppermute | solution.py:26
  165.7 1.3 collective-permute-start.19
  168.3 2.1 collective-permute-done.18
  171.1 4.2 %collective-permute-start.21 = (f32[3,1,8,128]{3,1,2,0:T(1,128)S(1)}, f32[3,1,8,128]{3,1,2,0:T(1,128)S(1)}, u32[]{:S(2)}, u32[]{:S(2)}) collective-permute-start(f32[3,1,8,128]{3,1,2,0:T(1,128)S(1)} %get-tuple-element.46), channel_id=1, source_target_pairs={{0,4},{4,8},{8,12},{12,16},{16,20},{20,24},{24,28},{1,5},{5,9},{9,... | collective-permute-start | bytes 36872 | tf_op jit(solution)/shard_map/ppermute | solution.py:23
  176.7 4.2 %collective-permute-done.20 = f32[3,1,8,128]{3,1,2,0:T(1,128)S(1)} collective-permute-done((f32[3,1,8,128]{3,1,2,0:T(1,128)S(1)}, f32[3,1,8,128]{3,1,2,0:T(1,128)S(1)}, u32[]{:S(2)}, u32[]{:S(2)}) %collective-permute-start.20) | collective-permute-done | bytes 12320 | tf_op jit(solution)/shard_map/ppermute | solution.py:26
  180.9 3.1 collective-permute-start.23
  185.4 2.7 collective-permute-done.22
  189.4 41.2 %all-reduce.9 = (f32[]{:T(128)}, f32[]{:T(128)}) all-reduce(f32[]{:T(128)} %get-tuple-element.7, f32[]{:T(128)} %get-tuple-element.6), channel_id=1, replica_groups=mesh['slab'=8,'grp'=4] {'slab','grp'}, use_global_device_ids=true, to_apply=%region_9.10 | all-reduce | flops 2 | bytes 16 | tf_op jit(solution)/shard_map/psum | solution.py:91
  232.6 4.4 %collective-permute-start.25 = (f32[3,1,8,128]{3,1,2,0:T(1,128)S(1)}, f32[3,1,8,128]{3,1,2,0:T(1,128)S(1)}, u32[]{:S(2)}, u32[]{:S(2)}) collective-permute-start(f32[3,1,8,128]{3,1,2,0:T(1,128)S(1)} %get-tuple-element.44), channel_id=1, source_target_pairs={{0,4},{4,8},{8,12},{12,16},{16,20},{20,24},{24,28},{1,5},{5,9},{9,... | collective-permute-start | bytes 36872 | tf_op jit(solution)/shard_map/ppermute | solution.py:23
  238.4 4.2 %collective-permute-done.24 = f32[3,1,8,128]{3,1,2,0:T(1,128)S(1)} collective-permute-done((f32[3,1,8,128]{3,1,2,0:T(1,128)S(1)}, f32[3,1,8,128]{3,1,2,0:T(1,128)S(1)}, u32[]{:S(2)}, u32[]{:S(2)}) %collective-permute-start.24) | collective-permute-done | bytes 12320 | tf_op jit(solution)/shard_map/ppermute | solution.py:26
  245.2 3.2 collective-permute-done.26
  249.7 41.6 %all-reduce.8 = (f32[]{:T(128)}, f32[]{:T(128)}) all-reduce(f32[]{:T(128)} %get-tuple-element.18, f32[]{:T(128)} %fusion.27), channel_id=1, replica_groups=mesh['slab'=8,'grp'=4] {'slab','grp'}, use_global_device_ids=true, to_apply=%region_13.14 | all-reduce | flops 2 | bytes 16 | tf_op jit(solution)/shard_map/psum | solution.py:91
  295.9 4.4 %collective-permute-start.29 = (f32[3,1,8,128]{3,1,2,0:T(1,128)S(1)}, f32[3,1,8,128]{3,1,2,0:T(1,128)S(1)}, u32[]{:S(2)}, u32[]{:S(2)}) collective-permute-start(f32[3,1,8,128]{3,1,2,0:T(1,128)S(1)} %get-tuple-element.42), channel_id=1, source_target_pairs={{0,4},{4,8},{8,12},{12,16},{16,20},{20,24},{24,28},{1,5},{5,9},{9,... | collective-permute-start | bytes 36872 | tf_op jit(solution)/shard_map/ppermute | solution.py:23
  301.8 4.2 %collective-permute-done.28 = f32[3,1,8,128]{3,1,2,0:T(1,128)S(1)} collective-permute-done((f32[3,1,8,128]{3,1,2,0:T(1,128)S(1)}, f32[3,1,8,128]{3,1,2,0:T(1,128)S(1)}, u32[]{:S(2)}, u32[]{:S(2)}) %collective-permute-start.28) | collective-permute-done | bytes 12320 | tf_op jit(solution)/shard_map/ppermute | solution.py:26
  307.3 1.5 collective-permute-start.30
  309.1 1.6 reshape.59
  313.6 2.1 copy.78
  315.6 1.9 reshape.63
  317.5 5.5 %all-to-all-start = ((f32[8,1,12288]{2,1,0:T(1,128)}), f32[8,1,12288]{2,1,0:T(1,128)S(1)}, u32[]{:S(2)}, u32[]{:S(2)}) async-start(f32[8,1,12288]{2,1,0:T(1,128)} %reshape.63), calls=%async_computation | async-start | bytes 786432 | tf_op jit(solution)/shard_map/all_to_all | solution.py:150
  323.8 9.6 %all-to-all-done = f32[8,1,12288]{2,1,0:T(1,128)S(1)} async-done(((f32[8,1,12288]{2,1,0:T(1,128)}), f32[8,1,12288]{2,1,0:T(1,128)S(1)}, u32[]{:S(2)}, u32[]{:S(2)}) %all-to-all-start) | async-done | bytes 393248 | tf_op jit(solution)/shard_map/all_to_all | solution.py:150
  333.8 2.3 reduce
  336.2 2.0 reshape.64
  338.2 3.5 copy.79
  341.7 2.4 all_to_all.16
  344.1 6.9 %slice.508 = f32[6,8,16,64]{3,2,1,0:T(8,128)S(1)} slice(f32[6,8,16,128]{3,2,1,0:T(8,128)S(1)} %all_to_all.16), slice={[0:6:1], [0:8:1], [0:16:1], [0:128:2]} | slice | bytes 393216 | tf_op jit(solution)/shard_map/slice | solution.py:95
  351.1 7.0 %slice.509 = f32[6,8,16,64]{3,2,1,0:T(8,128)S(1)} slice(f32[6,8,16,128]{3,2,1,0:T(8,128)S(1)} %all_to_all.16), slice={[0:6:1], [0:8:1], [0:16:1], [1:128:2]} | slice | bytes 393216 | tf_op jit(solution)/shard_map/slice | solution.py:96
  358.8 3.7 slice.514
  362.5 3.8 %slice.515 = f32[6,8,16,32]{3,2,1,0:T(8,128)S(1)} slice(f32[6,8,16,64]{3,2,1,0:T(8,128)S(1)} %fusion.11), slice={[0:6:1], [0:8:1], [0:16:1], [1:64:2]} | slice | bytes 196608 | tf_op jit(solution)/shard_map/slice | solution.py:96
  366.9 2.1 slice.520
  369.0 2.2 slice.521
  (118 shorter events, 38.1 us)
Async XLA Ops:
  0.6 2.8 copy-start.3
  0.6 9.0 %copy-start = (f32[3,16,8,128]{3,2,1,0:T(8,128)S(1)}, f32[3,16,8,128]{3,2,1,0:T(8,128)}, u32[]{:S(2)}) copy-start(f32[3,16,8,128]{3,2,1,0:T(8,128)} %param.27) | copy-start | bytes 589828
  1.7 26.7 %copy-start.1 = (f32[3,16,8,128]{3,2,1,0:T(8,128)S(1)}, f32[3,16,8,128]{3,2,1,0:T(8,128)}, u32[]{:S(2)}) copy-start(f32[3,16,8,128]{3,2,1,0:T(8,128)} %param.29) | copy-start | bytes 589828
  1.7 26.7 %copy-start.2 = (f32[3,16,8,128]{3,2,1,0:T(8,128)S(1)}, f32[3,16,8,128]{3,2,1,0:T(8,128)}, u32[]{:S(2)}) copy-start(f32[3,16,8,128]{3,2,1,0:T(8,128)} %param.28) | copy-start | bytes 589828
  1.7 26.7 %copy-start.5 = (f32[3]{0:T(128)S(1)}, f32[3]{0:T(128)}, u32[]{:S(2)}) copy-start(f32[3]{0:T(128)} %constant.9.clone) | copy-start | bytes 40
  1.7 26.7 %copy-start.6 = (f32[3]{0:T(128)S(1)}, f32[3]{0:T(128)}, u32[]{:S(2)}) copy-start(f32[3]{0:T(128)} %constant.8.clone) | copy-start | bytes 40
  1.8 26.7 %copy-start.7 = (f32[3]{0:T(128)S(1)}, f32[3]{0:T(128)}, u32[]{:S(2)}) copy-start(f32[3]{0:T(128)} %constant.7.clone) | copy-start | bytes 40
  3.5 12.8 %collective-permute-start.2 = (f32[1,8,128]{2,0,1:T(1,128)S(1)}, f32[1,8,128]{2,0,1:T(1,128)S(1)}, u32[]{:S(2)}, u32[]{:S(2)}) collective-permute-start(f32[1,8,128]{2,0,1:T(1,128)S(1)} %get-tuple-element.65), channel_id=1, source_target_pairs={{0,4},{4,8},{8,12},{12,16},{16,20},{20,24},{24,28},{1,5},{5,9},{9,... | collective-permute-start | bytes 12296 | tf_op jit(solution)/shard_map/ppermute | solution.py:23
  8.4 7.9 %collective-permute-start = (f32[1,8,128]{2,0,1:T(1,128)S(1)}, f32[1,8,128]{2,0,1:T(1,128)S(1)}, u32[]{:S(2)}, u32[]{:S(2)}) collective-permute-start(f32[1,8,128]{2,0,1:T(1,128)S(1)} %get-tuple-element.66), channel_id=1, source_target_pairs={{4,0},{8,4},{12,8},{16,12},{20,16},{24,20},{28,24},{5,1},{9,5},{13... | collective-permute-start | bytes 12296 | tf_op jit(solution)/shard_map/ppermute | solution.py:26
  9.7 9.2 %collective-permute-start.1 = (f32[3,1,8,128]{3,1,2,0:T(1,128)S(1)}, f32[3,1,8,128]{3,1,2,0:T(1,128)S(1)}, u32[]{:S(2)}, u32[]{:S(2)}) collective-permute-start(f32[3,1,8,128]{3,1,2,0:T(1,128)S(1)} %bitcast.71), channel_id=1, source_target_pairs={{4,0},{8,4},{12,8},{16,12},{20,16},{24,20},{28,24},{5,1},{9,5},{13... | collective-permute-start | bytes 36872 | tf_op jit(solution)/shard_map/ppermute | solution.py:26
  11.0 7.9 %collective-permute-start.3 = (f32[3,1,8,128]{3,1,2,0:T(1,128)S(1)}, f32[3,1,8,128]{3,1,2,0:T(1,128)S(1)}, u32[]{:S(2)}, u32[]{:S(2)}) collective-permute-start(f32[3,1,8,128]{3,1,2,0:T(1,128)S(1)} %bitcast.70), channel_id=1, source_target_pairs={{0,4},{4,8},{8,12},{12,16},{16,20},{20,24},{24,28},{1,5},{5,9},{9,... | collective-permute-start | bytes 36872 | tf_op jit(solution)/shard_map/ppermute | solution.py:23
  16.3 8.7 %collective-permute-start.6 = (f32[18,1,128]{2,0,1:T(8,128)S(1)}, f32[18,1,128]{2,0,1:T(8,128)S(1)}, u32[]{:S(2)}, u32[]{:S(2)}) collective-permute-start(f32[18,1,128]{2,0,1:T(8,128)S(1)} %get-tuple-element.59), channel_id=1, source_target_pairs={{0,1},{1,2},{2,3},{4,5},{5,6},{6,7},{8,9},{9,10},{10,11},{12,13},{... | collective-permute-start | bytes 27656 | tf_op jit(solution)/shard_map/ppermute | solution.py:23
  17.6 7.4 %collective-permute-start.4 = (f32[18,1,128]{2,0,1:T(8,128)S(1)}, f32[18,1,128]{2,0,1:T(8,128)S(1)}, u32[]{:S(2)}, u32[]{:S(2)}) collective-permute-start(f32[18,1,128]{2,0,1:T(8,128)S(1)} %get-tuple-element.60), channel_id=1, source_target_pairs={{1,0},{2,1},{3,2},{5,4},{6,5},{7,6},{9,8},{10,9},{11,10},{13,12},{... | collective-permute-start | bytes 27656 | tf_op jit(solution)/shard_map/ppermute | solution.py:26
  18.9 6.4 %collective-permute-start.7 = (f32[3,18,1,128]{3,1,2,0:T(8,128)S(1)}, f32[3,18,1,128]{3,1,2,0:T(8,128)S(1)}, u32[]{:S(2)}, u32[]{:S(2)}) collective-permute-start(f32[3,18,1,128]{3,1,2,0:T(8,128)S(1)} %get-tuple-element.40), channel_id=1, source_target_pairs={{0,1},{1,2},{2,3},{4,5},{5,6},{6,7},{8,9},{9,10},{10,11},{12,13},{... | collective-permute-start | bytes 82952 | tf_op jit(solution)/shard_map/ppermute | solution.py:23
  23.7 4.3 %collective-permute-start.5 = (f32[3,18,1,128]{3,1,2,0:T(8,128)S(1)}, f32[3,18,1,128]{3,1,2,0:T(8,128)S(1)}, u32[]{:S(2)}, u32[]{:S(2)}) collective-permute-start(f32[3,18,1,128]{3,1,2,0:T(8,128)S(1)} %get-tuple-element.41), channel_id=1, source_target_pairs={{1,0},{2,1},{3,2},{5,4},{6,5},{7,6},{9,8},{10,9},{11,10},{13,12},{... | collective-permute-start | bytes 82952 | tf_op jit(solution)/shard_map/ppermute | solution.py:26
  28.8 6.2 %collective-permute-start.9 = (f32[3,1,8,128]{3,1,2,0:T(1,128)S(1)}, f32[3,1,8,128]{3,1,2,0:T(1,128)S(1)}, u32[]{:S(2)}, u32[]{:S(2)}) collective-permute-start(f32[3,1,8,128]{3,1,2,0:T(1,128)S(1)} %get-tuple-element.52), channel_id=1, source_target_pairs={{0,4},{4,8},{8,12},{12,16},{16,20},{20,24},{24,28},{1,5},{5,9},{9,... | collective-permute-start | bytes 36872 | tf_op jit(solution)/shard_map/ppermute | solution.py:23
  33.6 5.6 %collective-permute-start.8 = (f32[3,1,8,128]{3,1,2,0:T(1,128)S(1)}, f32[3,1,8,128]{3,1,2,0:T(1,128)S(1)}, u32[]{:S(2)}, u32[]{:S(2)}) collective-permute-start(f32[3,1,8,128]{3,1,2,0:T(1,128)S(1)} %get-tuple-element.53), channel_id=1, source_target_pairs={{4,0},{8,4},{12,8},{16,12},{20,16},{24,20},{28,24},{5,1},{9,5},{13... | collective-permute-start | bytes 36872 | tf_op jit(solution)/shard_map/ppermute | solution.py:26
  39.2 4.5 %collective-permute-start.11 = (f32[3,18,1,128]{3,1,2,0:T(8,128)S(1)}, f32[3,18,1,128]{3,1,2,0:T(8,128)S(1)}, u32[]{:S(2)}, u32[]{:S(2)}) collective-permute-start(f32[3,18,1,128]{3,1,2,0:T(8,128)S(1)} %get-tuple-element.38), channel_id=1, source_target_pairs={{0,1},{1,2},{2,3},{4,5},{5,6},{6,7},{8,9},{9,10},{10,11},{12,13},{... | collective-permute-start | bytes 82952 | tf_op jit(solution)/shard_map/ppermute | solution.py:23
  42.4 4.0 %collective-permute-start.10 = (f32[3,18,1,128]{3,1,2,0:T(8,128)S(1)}, f32[3,18,1,128]{3,1,2,0:T(8,128)S(1)}, u32[]{:S(2)}, u32[]{:S(2)}) collective-permute-start(f32[3,18,1,128]{3,1,2,0:T(8,128)S(1)} %get-tuple-element.39), channel_id=1, source_target_pairs={{1,0},{2,1},{3,2},{5,4},{6,5},{7,6},{9,8},{10,9},{11,10},{13,12},{... | collective-permute-start | bytes 82952 | tf_op jit(solution)/shard_map/ppermute | solution.py:26
  92.4 5.8 %collective-permute-start.13 = (f32[3,1,8,128]{3,1,2,0:T(1,128)S(1)}, f32[3,1,8,128]{3,1,2,0:T(1,128)S(1)}, u32[]{:S(2)}, u32[]{:S(2)}) collective-permute-start(f32[3,1,8,128]{3,1,2,0:T(1,128)S(1)} %get-tuple-element.50), channel_id=1, source_target_pairs={{0,4},{4,8},{8,12},{12,16},{16,20},{20,24},{24,28},{1,5},{5,9},{9,... | collective-permute-start | bytes 36872 | tf_op jit(solution)/shard_map/ppermute | solution.py:23
  96.8 5.6 %collective-permute-start.12 = (f32[3,1,8,128]{3,1,2,0:T(1,128)S(1)}, f32[3,1,8,128]{3,1,2,0:T(1,128)S(1)}, u32[]{:S(2)}, u32[]{:S(2)}) collective-permute-start(f32[3,1,8,128]{3,1,2,0:T(1,128)S(1)} %get-tuple-element.51), channel_id=1, source_target_pairs={{4,0},{8,4},{12,8},{16,12},{20,16},{24,20},{28,24},{5,1},{9,5},{13... | collective-permute-start | bytes 36872 | tf_op jit(solution)/shard_map/ppermute | solution.py:26
  102.4 2.6 collective-permute-start.15
  103.7 3.4 collective-permute-start.14
  155.7 5.8 %collective-permute-start.17 = (f32[3,1,8,128]{3,1,2,0:T(1,128)S(1)}, f32[3,1,8,128]{3,1,2,0:T(1,128)S(1)}, u32[]{:S(2)}, u32[]{:S(2)}) collective-permute-start(f32[3,1,8,128]{3,1,2,0:T(1,128)S(1)} %get-tuple-element.48), channel_id=1, source_target_pairs={{0,4},{4,8},{8,12},{12,16},{16,20},{20,24},{24,28},{1,5},{5,9},{9,... | collective-permute-start | bytes 36872 | tf_op jit(solution)/shard_map/ppermute | solution.py:23
  160.1 5.6 %collective-permute-start.16 = (f32[3,1,8,128]{3,1,2,0:T(1,128)S(1)}, f32[3,1,8,128]{3,1,2,0:T(1,128)S(1)}, u32[]{:S(2)}, u32[]{:S(2)}) collective-permute-start(f32[3,1,8,128]{3,1,2,0:T(1,128)S(1)} %get-tuple-element.49), channel_id=1, source_target_pairs={{4,0},{8,4},{12,8},{16,12},{20,16},{24,20},{28,24},{5,1},{9,5},{13... | collective-permute-start | bytes 36872 | tf_op jit(solution)/shard_map/ppermute | solution.py:26
  165.7 2.6 collective-permute-start.19
  167.0 3.4 collective-permute-start.18
  171.1 5.6 %collective-permute-start.21 = (f32[3,1,8,128]{3,1,2,0:T(1,128)S(1)}, f32[3,1,8,128]{3,1,2,0:T(1,128)S(1)}, u32[]{:S(2)}, u32[]{:S(2)}) collective-permute-start(f32[3,1,8,128]{3,1,2,0:T(1,128)S(1)} %get-tuple-element.46), channel_id=1, source_target_pairs={{0,4},{4,8},{8,12},{12,16},{16,20},{20,24},{24,28},{1,5},{5,9},{9,... | collective-permute-start | bytes 36872 | tf_op jit(solution)/shard_map/ppermute | solution.py:23
  175.3 5.6 %collective-permute-start.20 = (f32[3,1,8,128]{3,1,2,0:T(1,128)S(1)}, f32[3,1,8,128]{3,1,2,0:T(1,128)S(1)}, u32[]{:S(2)}, u32[]{:S(2)}) collective-permute-start(f32[3,1,8,128]{3,1,2,0:T(1,128)S(1)} %get-tuple-element.47), channel_id=1, source_target_pairs={{4,0},{8,4},{12,8},{16,12},{20,16},{24,20},{28,24},{5,1},{9,5},{13... | collective-permute-start | bytes 36872 | tf_op jit(solution)/shard_map/ppermute | solution.py:26
  180.9 4.5 %collective-permute-start.23 = (f32[3,18,1,128]{3,1,2,0:T(8,128)S(1)}, f32[3,18,1,128]{3,1,2,0:T(8,128)S(1)}, u32[]{:S(2)}, u32[]{:S(2)}) collective-permute-start(f32[3,18,1,128]{3,1,2,0:T(8,128)S(1)} %get-tuple-element.32), channel_id=1, source_target_pairs={{0,1},{1,2},{2,3},{4,5},{5,6},{6,7},{8,9},{9,10},{10,11},{12,13},{... | collective-permute-start | bytes 82952 | tf_op jit(solution)/shard_map/ppermute | solution.py:23
  184.1 124.7 %copy-start.10 = (s32[4,2,32]{2,1,0:T(2,128)S(1)}, s32[4,2,32]{2,1,0:T(2,128)}, u32[]{:S(2)}) copy-start(s32[4,2,32]{2,1,0:T(2,128)} %param.32) | copy-start | bytes 3076
  184.1 4.0 %collective-permute-start.22 = (f32[3,18,1,128]{3,1,2,0:T(8,128)S(1)}, f32[3,18,1,128]{3,1,2,0:T(8,128)S(1)}, u32[]{:S(2)}, u32[]{:S(2)}) collective-permute-start(f32[3,18,1,128]{3,1,2,0:T(8,128)S(1)} %get-tuple-element.33), channel_id=1, source_target_pairs={{1,0},{2,1},{3,2},{5,4},{6,5},{7,6},{9,8},{10,9},{11,10},{13,12},{... | collective-permute-start | bytes 82952 | tf_op jit(solution)/shard_map/ppermute | solution.py:26
  232.6 5.8 %collective-permute-start.25 = (f32[3,1,8,128]{3,1,2,0:T(1,128)S(1)}, f32[3,1,8,128]{3,1,2,0:T(1,128)S(1)}, u32[]{:S(2)}, u32[]{:S(2)}) collective-permute-start(f32[3,1,8,128]{3,1,2,0:T(1,128)S(1)} %get-tuple-element.44), channel_id=1, source_target_pairs={{0,4},{4,8},{8,12},{12,16},{16,20},{20,24},{24,28},{1,5},{5,9},{9,... | collective-permute-start | bytes 36872 | tf_op jit(solution)/shard_map/ppermute | solution.py:23
  237.0 5.6 %collective-permute-start.24 = (f32[3,1,8,128]{3,1,2,0:T(1,128)S(1)}, f32[3,1,8,128]{3,1,2,0:T(1,128)S(1)}, u32[]{:S(2)}, u32[]{:S(2)}) collective-permute-start(f32[3,1,8,128]{3,1,2,0:T(1,128)S(1)} %get-tuple-element.45), channel_id=1, source_target_pairs={{4,0},{8,4},{12,8},{16,12},{20,16},{24,20},{28,24},{5,1},{9,5},{13... | collective-permute-start | bytes 36872 | tf_op jit(solution)/shard_map/ppermute | solution.py:26
  242.6 2.6 collective-permute-start.27
  243.9 4.5 %collective-permute-start.26 = (f32[3,18,1,128]{3,1,2,0:T(8,128)S(1)}, f32[3,18,1,128]{3,1,2,0:T(8,128)S(1)}, u32[]{:S(2)}, u32[]{:S(2)}) collective-permute-start(f32[3,18,1,128]{3,1,2,0:T(8,128)S(1)} %get-tuple-element.31), channel_id=1, source_target_pairs={{1,0},{2,1},{3,2},{5,4},{6,5},{7,6},{9,8},{10,9},{11,10},{13,12},{... | collective-permute-start | bytes 82952 | tf_op jit(solution)/shard_map/ppermute | solution.py:26
  295.9 5.8 %collective-permute-start.29 = (f32[3,1,8,128]{3,1,2,0:T(1,128)S(1)}, f32[3,1,8,128]{3,1,2,0:T(1,128)S(1)}, u32[]{:S(2)}, u32[]{:S(2)}) collective-permute-start(f32[3,1,8,128]{3,1,2,0:T(1,128)S(1)} %get-tuple-element.42), channel_id=1, source_target_pairs={{0,4},{4,8},{8,12},{12,16},{16,20},{20,24},{24,28},{1,5},{5,9},{9,... | collective-permute-start | bytes 36872 | tf_op jit(solution)/shard_map/ppermute | solution.py:23
  300.4 10.9 %copy-start.8 = (f32[16,16,1,1]{1,0,3,2:T(8,128)S(1)}, f32[16,16,1,1]{1,0,3,2:T(8,128)}, u32[]{:S(2)}) copy-start(f32[16,16,1,1]{1,0,3,2:T(8,128)} %constant.55) | copy-start | bytes 3076
  300.4 5.6 %collective-permute-start.28 = (f32[3,1,8,128]{3,1,2,0:T(1,128)S(1)}, f32[3,1,8,128]{3,1,2,0:T(1,128)S(1)}, u32[]{:S(2)}, u32[]{:S(2)}) collective-permute-start(f32[3,1,8,128]{3,1,2,0:T(1,128)S(1)} %get-tuple-element.43), channel_id=1, source_target_pairs={{4,0},{8,4},{12,8},{16,12},{20,16},{24,20},{28,24},{5,1},{9,5},{13... | collective-permute-start | bytes 36872 | tf_op jit(solution)/shard_map/ppermute | solution.py:26
  306.0 4.8 %collective-permute-start.31 = (f32[3,18,1,128]{3,1,2,0:T(8,128)S(1)}, f32[3,18,1,128]{3,1,2,0:T(8,128)S(1)}, u32[]{:S(2)}, u32[]{:S(2)}) collective-permute-start(f32[3,18,1,128]{3,1,2,0:T(8,128)S(1)} %get-tuple-element.28), channel_id=1, source_target_pairs={{0,1},{1,2},{2,3},{4,5},{5,6},{6,7},{8,9},{9,10},{10,11},{12,13},{... | collective-permute-start | bytes 82952 | tf_op jit(solution)/shard_map/ppermute | solution.py:23
  307.3 3.5 collective-permute-start.30
  308.8 3.0 copy-start.9
  309.1 3.2 copy-start.4
  317.5 15.8 %all-to-all-start = ((f32[8,1,12288]{2,1,0:T(1,128)}), f32[8,1,12288]{2,1,0:T(1,128)S(1)}, u32[]{:S(2)}, u32[]{:S(2)}) async-start(f32[8,1,12288]{2,1,0:T(1,128)} %reshape.63), calls=%async_computation | async-start | bytes 786432 | tf_op jit(solution)/shard_map/all_to_all | solution.py:150
where the time goes:
time: 377 us; the launch traced here: 373 us
  blocking collectives  168 us (45%)
  starting transfers between devices  80.6 us (21%)
  waiting for transfers between devices  50.9 us (14%)
  local copies, waits for them, and re-layouts  43.8 us (12%)
  other arithmetic  13.9 us (4%)
  between operations  13.3 us (4%)
    psum x4, blocking collectives, paired_sum(): lax.psum((jnp.sum(residual * residual), jnp.sum(residual * image)), ('sla...  168 us
    ppermute x16, starting transfers between devices, with_halo(): lax.ppermute(lax.slice_in_dim(block, block.shape[dim] - width, None, axis...  54.2 us
    ppermute x16, waiting for transfers between devices, with_halo(): lax.ppermute(lax.slice_in_dim(block, 0, width, axis=dim), axis, backward)  40.8 us
    ppermute x16, starting transfers between devices, with_halo(): lax.ppermute(lax.slice_in_dim(block, 0, width, axis=dim), axis, backward)  20.9 us
    slice x3, local copies, waits for them, and re-layouts, lift(): odd = signal[..., 1::2]  12.9 us
    slice x3, local copies, waits for them, and re-layouts, lift(): even = signal[..., 0::2]  12.6 us
    all_to_all x1, waiting for transfers between devices, body(): lax.all_to_all(moved, 'slab', split_axis=2, concat_axis=3, tiled=True)  9.58 us
  transfers between devices with their start and end apart: 33, of which 19 were waited for; matrix products, arithmetic and copies ran while one was open for 1% of the time, Pallas kernels for 0%

commit v1 on v0

--- a/solution.py
+++ b/solution.py
@@ -2,6 +2,8 @@
 import jax.numpy as jnp
 import numpy as np
 from jax import lax
+from jax.experimental import pallas as pl
+from jax.experimental.pallas import tpu as pltpu
 from jax.sharding import PartitionSpec as P
 
 STEPS = 2
@@ -152,9 +154,539 @@
     return (u_now, coeffs)
 
 
+MESH = pl.DeviceIdType.MESH
+HALO = 4
+REACH = 3
+SHEAR_REST = SPRING_NORMAL - SPRING_SHEAR
+
+
+def wavelet_table(count):
+    table = np.kron(np.eye(count // 4), cosine_table())
+    pieces = []
+    approx = table
+    for level_index in range(LEVELS):
+        even, odd = approx[0::2], approx[1::2]
+        detail = odd - 0.5 * (even + np.roll(even, -1, axis=0))
+        approx = even + 0.25 * (np.roll(detail, 1, axis=0) + detail)
+        pieces.insert(0, detail)
+    return np.concatenate([approx] + pieces, axis=0)
+
+
+def sub_index():
+    return lax.broadcasted_iota(jnp.int32, (8, 128), 0)
+
+
+def lane_index():
+    return lax.broadcasted_iota(jnp.int32, (8, 128), 1)
+
+
+def up_y(a, b):
+    ra, rb = pltpu.roll(a, 7, 0), pltpu.roll(b, 7, 0)
+    last = sub_index() == 7
+    return jnp.where(last, rb, ra), jnp.where(last, ra, rb)
+
+
+def down_y(a, b):
+    ra, rb = pltpu.roll(a, 1, 0), pltpu.roll(b, 1, 0)
+    first = sub_index() == 0
+    return jnp.where(first, rb, ra), jnp.where(first, ra, rb)
+
+
+def up_z(v):
+    return pltpu.roll(v, 127, 1)
+
+
+def down_z(v):
+    return pltpu.roll(v, 1, 1)
+
+
+def total(v):
+    return jnp.sum(jnp.sum(v, axis=0, keepdims=True), axis=1, keepdims=True)
+
+
+def kernel(ns, ng, u_ref, p_ref, f_ref, k_ref, br_ref, fl_ref, ez_ref, cz_ref, gt_ref,
+           disp_ref, coef_ref,
+           e1a, e1b, s1, h1, e2a, e2b, s2, h2, rqa, rqb, e3a, s3, h3,
+           u1a, u1b, carry, dga, dgb, kca, kcb, gath, rows, outb, inb,
+           send1, recv1, send2, recv2, send3, recv3, asend, arecv, tsend, trecv):
+    X, Y = u_ref.shape[1], u_ref.shape[2]
+    si, gi = lax.axis_index("slab"), lax.axis_index("grp")
+    me = si * ng + gi
+    count = ns * ng
+    barrier = pltpu.get_barrier_semaphore()
+
+    def greet(i, _):
+        other = lax.rem(me + i, count)
+        pl.semaphore_signal(barrier, inc=1, device_id=(other // ng, lax.rem(other, ng)), device_id_type=MESH)
+        return 0
+
+    lax.fori_loop(1, count, greet, 0)
+
+    sub, lane = sub_index(), lane_index()
+    upper = sub < 4
+
+    steps = [(-1, 0), (1, 0), (0, -1), (0, 1), (-1, -1), (-1, 1), (1, -1), (1, 1)]
+
+    def inside(ds, dg):
+        ok = None
+        if ds:
+            ok = (si >= 1) if ds < 0 else (si <= ns - 2)
+        if dg:
+            more = (gi >= 1) if dg < 0 else (gi <= ng - 2)
+            ok = more if ok is None else jnp.logical_and(ok, more)
+        return ok
+
+    def copies(ea, dst_a, stage, land, send, recv):
+        half = X // 2
+        edge = HALO // 2
+        made = []
+        for at, (ds, dg) in enumerate(steps):
+            if dg == 0:
+                if ds < 0:
+                    source = ea.at[:, pl.ds(HALO, REACH)]
+                    target = dst_a.at[:, pl.ds(HALO + X, REACH)]
+                else:
+                    source = ea.at[:, pl.ds(HALO + X - REACH, REACH)]
+                    target = dst_a.at[:, pl.ds(HALO - REACH, REACH)]
+            else:
+                side = 0 if dg < 0 else 1
+                if ds == 0:
+                    source, target = stage.at[side], land.at[side, :, pl.ds(edge, half)]
+                elif ds < 0:
+                    source = stage.at[side, :, pl.ds(0, edge)]
+                    target = land.at[side, :, pl.ds(edge + half, edge)]
+                else:
+                    source = stage.at[side, :, pl.ds(half - edge, edge)]
+                    target = land.at[side, :, pl.ds(0, edge)]
+            made.append((ds, dg, pltpu.make_async_remote_copy(
+                src_ref=source, dst_ref=target, send_sem=send.at[at], recv_sem=recv.at[at ^ 1 if at < 4 else 11 - at],
+                device_id=(si + ds, gi + dg), device_id_type=MESH)))
+        return made
+
+    def begin(made):
+        for ds, dg, copy in made:
+            @pl.when(inside(ds, dg))
+            def _():
+                copy.start()
+
+    def finish_recv(made, recv):
+        for at, (ds, dg) in enumerate(steps):
+            back = made[at ^ 1 if at < 4 else 11 - at][2]
+
+            @pl.when(inside(ds, dg))
+            def _():
+                back.wait_recv()
+
+    def finish_send(made):
+        for ds, dg, copy in made:
+            @pl.when(inside(ds, dg))
+            def _():
+                copy.wait_send()
+
+    def blank(dst_a, land):
+        zero_a = jnp.zeros((dst_a.shape[0], HALO) + dst_a.shape[2:], jnp.float32)
+        half, edge = X // 2, HALO // 2
+        zero_l = jnp.zeros((land.shape[1], edge, 8, 128), jnp.float32)
+
+        @pl.when(si == 0)
+        def _():
+            dst_a[:, pl.ds(0, HALO)] = zero_a
+            for side in range(2):
+                land[side, :, pl.ds(0, edge)] = zero_l
+
+        @pl.when(si == ns - 1)
+        def _():
+            dst_a[:, pl.ds(HALO + X, HALO)] = zero_a
+            for side in range(2):
+                land[side, :, pl.ds(edge + half, edge)] = zero_l
+
+        for side, edge_here in ((0, gi == ng - 1), (1, gi == 0)):
+            @pl.when(edge_here)
+            def _(side=side):
+                land[side] = jnp.zeros(land.shape[1:], jnp.float32)
+
+    def pack(stage, ch, pair, even, odd):
+        stage[0, ch, pair] = jnp.where(upper, even, pltpu.roll(odd, 4, 0))
+        stage[1, ch, pair] = jnp.where(upper, pltpu.roll(even, 4, 0), odd)
+
+    def unpack(land, ch, pair):
+        high, low = land[0, ch, pair], land[1, ch, pair]
+        return (jnp.where(upper, high, pltpu.roll(low, 4, 0)),
+                jnp.where(upper, pltpu.roll(high, 4, 0), low))
+
+    def spread_rows(mask):
+        wide = jnp.dot(mask.astype(jnp.float32), ez_ref[...], preferred_element_type=jnp.float32)
+        return jnp.where(upper, jnp.broadcast_to(wide[0:1], (8, 128)), jnp.broadcast_to(wide[1:2], (8, 128)))
+
+    for bx in range(X // 4):
+        cut = 1.0 - CRACK_CUT * spread_rows(br_ref[bx])
+        flag = spread_rows(fl_ref[bx])
+        for at in range(4):
+            x = bx * 4 + at
+            w = k_ref[x] * cut
+            e1a[6, HALO + x] = w
+            carry[x] = flag * w
+
+    def own(i, _):
+        for c in range(3):
+            tiles = []
+            for o in range(2):
+                x = 2 * i + o
+                u = u_ref[c, x]
+                f = f_ref[c, x]
+                rhs = MASS_TERM * (2.0 * u - p_ref[c, x]) + f
+                e1a[c, HALO + x] = u
+                e1a[3 + c, HALO + x] = rhs
+                e2a[c, HALO + x] = f
+                tiles.append((u, rhs, f))
+            pack(s1, c, i, tiles[0][0], tiles[1][0])
+            pack(s1, 3 + c, i, tiles[0][1], tiles[1][1])
+            pack(s2, c, i, tiles[0][2], tiles[1][2])
+        pack(s1, 6, i, e1a[6, HALO + 2 * i], e1a[6, HALO + 2 * i + 1])
+        return 0
+
+    lax.fori_loop(0, X // 2, own, 0)
+    blank(e1a, h1)
+    blank(e2a, h2)
+    blank(e3a, h3)
+
+    first = copies(e1a, e1a, s1, h1, send1, recv1)
+    second = copies(e2a, e2a, s2, h2, send2, recv2)
+    third = copies(rqa, e3a, s3, h3, send3, recv3)
+    pl.semaphore_wait(barrier, count - 1)
+    begin(first)
+    finish_recv(first, recv1)
+    begin(second)
+
+    def open1(i, _):
+        for ch in range(7):
+            e1b[ch, 2 * i], e1b[ch, 2 * i + 1] = unpack(h1, ch, i)
+        return 0
+
+    lax.fori_loop(0, (X + 2 * HALO) // 2, open1, 0)
+
+    def link(w, other):
+        return jnp.where(jnp.minimum(w, other) > 0.0, 0.5 * (w + other), 0.0)
+
+    not_last, not_first = lane < 127, lane > 0
+
+    def coefficients(x, _):
+        wa, wb = e1a[6, x], e1b[6, x]
+        ya, yb = up_y(wa, wb)
+        da, db = down_y(wa, wb)
+        for w, wu, wd, yu, yd, dg, kc in (
+            (wa, e1a[6, x + 1], e1a[6, x - 1], ya, da, dga, kca),
+            (wb, e1b[6, x + 1], e1b[6, x - 1], yb, db, dgb, kcb),
+        ):
+            zu = jnp.where(not_last, up_z(w), 0.0)
+            zd = jnp.where(not_first, down_z(w), 0.0)
+            kc[0, x] = link(w, wu)
+            kc[1, x] = link(w, yu)
+            kc[2, x] = link(w, yd)
+            kc[3, x] = link(w, zu)
+            kc[4, x] = link(w, zd)
+            sx = w + 0.5 * (wu + wd)
+            sy = w + 0.5 * (yu + yd)
+            sz = w + 0.5 * (zu + zd)
+            every = MASS_TERM + SPRING_SHEAR * (sx + sy + sz)
+            dg[0, x] = every + SHEAR_REST * sx
+            dg[1, x] = every + SHEAR_REST * sy
+            dg[2, x] = every + SHEAR_REST * sz
+        return 0
+
+    kca[0, HALO - REACH] = link(e1a[6, HALO - REACH], e1a[6, HALO - REACH + 1])
+    kcb[0, HALO - REACH] = link(e1b[6, HALO - REACH], e1b[6, HALO - REACH + 1])
+    lax.fori_loop(HALO - 2, HALO + X + 2, coefficients, 0)
+
+    def operate(x, va, vb, base):
+        result = []
+        coef = [[kc[j, x] for j in range(5)] + [kc[0, x - 1]] for kc in (kca, kcb)]
+        for c in range(3):
+            a, b = va[base + c, x], vb[base + c, x]
+            ua, ub = up_y(a, b)
+            la, lb = down_y(a, b)
+            pair = []
+            for v, ref, u, l, k, dg in ((a, va, ua, la, coef[0], dga), (b, vb, ub, lb, coef[1], dgb)):
+                parts = (
+                    k[0] * ref[base + c, x + 1] + k[5] * ref[base + c, x - 1],
+                    k[1] * u + k[2] * l,
+                    k[3] * up_z(v) + k[4] * down_z(v),
+                )
+                every = parts[0] + parts[1] + parts[2]
+                pair.append(dg[c, x] * v - (SPRING_SHEAR * every + SHEAR_REST * parts[c]))
+            result.append(pair)
+        return result
+
+    def solve(step, va, vb, rhs_of):
+        def residual(x, _):
+            image = operate(x, va, vb, 0)
+            for c in range(3):
+                ra, rb = rhs_of(c, x)
+                rqa[c, x] = ra - image[c][0]
+                rqb[c, x] = rb - image[c][1]
+            return 0
+
+        lax.fori_loop(HALO - 2, HALO + X + 2, residual, 0)
+
+        def apply(x, _):
+            image = operate(x, rqa, rqb, 0)
+            for c in range(3):
+                rqa[3 + c, x] = image[c][0]
+                rqb[3 + c, x] = image[c][1]
+            return 0
+
+        lax.fori_loop(HALO - 1, HALO + X + 1, apply, 0)
+
+        def products(x, sums):
+            rr, rq = sums
+            for c in range(3):
+                r, q = rqa[c, x], rqa[3 + c, x]
+                rr, rq = rr + r * r, rq + r * q
+            return rr, rq
+
+        zero = jnp.zeros((8, 128), jnp.float32)
+        rr, rq = lax.fori_loop(HALO, HALO + X, products, (zero, zero))
+        rr, rq = total(rr), total(rq)
+        mu = jnp.where(rr > 0.0, rq / jnp.where(rr > 0.0, rr, 1.0), 0.0)
+
+        def centred(x, sums):
+            ww, wr, mix, wt = sums
+            image = operate(x, rqa, rqb, 3)
+            for c in range(3):
+                r, q, s = rqa[c, x], rqa[3 + c, x], image[c][0]
+                w, t = q - mu * r, s - mu * q
+                ww, wr, mix, wt = ww + w * w, wr + w * r, mix + (r * t + w * q), wt + w * t
+            return ww, wr, mix, wt
+
+        sums = lax.fori_loop(HALO, HALO + X, centred, (zero,) * 4)
+        ww, wr, mix, wt = [total(v) for v in sums]
+        one = lax.broadcasted_iota(jnp.int32, (1, 128), 1)
+        row = jnp.zeros((1, 128), jnp.float32)
+        for at, value in enumerate((rr, rq, mu, ww, wr, mix, wt)):
+            row = jnp.where(one == at, value, row)
+        gath[step, me] = row
+
+        def share(i, _):
+            other = lax.rem(me + i, count)
+            pltpu.make_async_remote_copy(
+                src_ref=gath.at[step, me], dst_ref=gath.at[step, me], send_sem=asend.at[step], recv_sem=arecv.at[step],
+                device_id=(other // ng, lax.rem(other, ng)), device_id_type=MESH).start()
+            return 0
+
+        lax.fori_loop(1, count, share, 0)
+
+    def collect(step):
+        block = gath.at[step, pl.ds(0, count - 1)]
+        pltpu.make_async_copy(block, block, arecv.at[step]).wait()
+        table = gath[step].reshape(count, 128)
+        rr, rq, mu, ww, wr, mix, wt = [table[:, at:at + 1] for at in range(7)]
+
+        def down(v):
+            return jnp.sum(v, axis=0, keepdims=True)
+
+        norm = down(rr)
+        alpha = norm / down(rq)
+        rest = 1.0 - alpha * mu
+        after = down(alpha * alpha * ww - 2.0 * alpha * rest * wr + rest * rest * rr)
+        curved = down(rest * rest * rq - alpha * rest * mix + alpha * alpha * wt)
+        ratio = after / norm
+        beta = after / (curved - ratio * after / alpha)
+        return alpha + beta * (1.0 + ratio), -beta * alpha
+
+    def drain(step):
+        block = gath.at[step, pl.ds(0, count - 1)]
+        pltpu.make_async_copy(block, block, asend.at[step]).wait()
+
+    solve(0, e1a, e1b, lambda c, x: (e1a[3 + c, x], e1b[3 + c, x]))
+
+    def pack3(i, _):
+        for ch in range(6):
+            pack(s3, ch, i, rqa[ch, HALO + 2 * i], rqa[ch, HALO + 2 * i + 1])
+        return 0
+
+    lax.fori_loop(0, X // 2, pack3, 0)
+    begin(third)
+
+    finish_recv(second, recv2)
+
+    def open2(i, _):
+        for ch in range(3):
+            e2b[ch, 2 * i], e2b[ch, 2 * i + 1] = unpack(h2, ch, i)
+        return 0
+
+    lax.fori_loop(0, (X + 2 * HALO) // 2, open2, 0)
+    finish_recv(third, recv3)
+    c0, c1 = collect(0)
+
+    def step_b(i, _):
+        for c in range(3):
+            r0, r1 = unpack(h3, c, i)
+            q0, q1 = unpack(h3, 3 + c, i)
+            u1b[c, 2 * i] = e1b[c, 2 * i] + (c0 * r0 + c1 * q0)
+            u1b[c, 2 * i + 1] = e1b[c, 2 * i + 1] + (c0 * r1 + c1 * q1)
+        return 0
+
+    lax.fori_loop(0, (X + 2 * HALO) // 2, step_b, 0)
+
+    def step_a(x, _):
+        for c in range(3):
+            u1a[c, x] = e1a[c, x] + (c0 * rqa[c, x] + c1 * rqa[3 + c, x])
+        return 0
+
+    lax.fori_loop(HALO, HALO + X, step_a, 0)
+    for x in list(range(HALO - REACH, HALO)) + list(range(HALO + X, HALO + X + REACH)):
+        for c in range(3):
+            u1a[c, x] = e1a[c, x] + (c0 * e3a[c, x] + c1 * e3a[3 + c, x])
+    finish_send(first)
+    finish_send(second)
+    finish_send(third)
+
+    def rhs2(c, x):
+        return (MASS_TERM * (2.0 * u1a[c, x] - e1a[c, x]) + e2a[c, x],
+                MASS_TERM * (2.0 * u1b[c, x] - e1b[c, x]) + e2b[c, x])
+
+    solve(1, u1a, u1b, rhs2)
+    c0, c1 = collect(1)
+
+    def step2(x, _):
+        for c in range(3):
+            va = u1a[c, x] + (c0 * rqa[c, x] + c1 * rqa[3 + c, x])
+            vb = u1b[c, x] + (c0 * rqb[c, x] + c1 * rqb[3 + c, x])
+            u1a[c, x] = va
+            u1b[c, x] = vb
+        return 0
+
+    lax.fori_loop(HALO - 1, HALO + X + 1, step2, 0)
+
+    def finals(x, _):
+        at = x - HALO
+        scale = SPRING_NORMAL * carry[at] * 0.5
+        values = [u1a[c, x] for c in range(3)]
+        for c in range(3):
+            disp_ref[c, at] = values[c]
+        dx = u1a[0, x + 1] - u1a[0, x - 1]
+        dy = up_y(values[1], u1b[1, x])[0] - down_y(values[1], u1b[1, x])[0]
+        dz = jnp.where(not_last, up_z(values[2]), 0.0) - jnp.where(not_first, down_z(values[2]), 0.0)
+        for c, v in enumerate(values + [scale * dx, scale * dy, scale * dz]):
+            rows[c, pl.ds(at, 8, stride=X), :] = v
+        return 0
+
+    lax.fori_loop(HALO, HALO + X, finals, 0)
+
+    zrows = coef_ref.shape[2]
+
+    def transform(c, _):
+        turned = lax.dot_general(cz_ref[...], rows[c], (((1,), (1,)), ((), ())),
+                                 precision=lax.Precision.HIGHEST, preferred_element_type=jnp.float32)
+        for j in range(ns):
+            outb[j, c] = turned[j * zrows:(j + 1) * zrows]
+        return 0
+
+    lax.fori_loop(0, 6, transform, 0)
+
+    def trade(i):
+        to = lax.rem(si + i, ns)
+        return pltpu.make_async_remote_copy(
+            src_ref=outb.at[to], dst_ref=inb.at[i], send_sem=tsend.at[i], recv_sem=trecv.at[i],
+            device_id=(to, gi), device_id_type=MESH)
+
+    trades = [None] + [trade(i) for i in range(1, ns)]
+    for i in range(1, ns):
+        trades[i].start()
+    inb[0] = outb[si]
+    for i in range(1, ns):
+        trades[i].wait_recv()
+
+    zlane = lax.broadcasted_iota(jnp.int32, (zrows, 128), 1)
+    c1t, c3t = float(np.sqrt(0.5) * np.cos(np.pi / 8)), float(np.sqrt(0.5) * np.cos(3 * np.pi / 8))
+
+    def gather_back(c, _):
+        pieces = [None] * Y
+        for y in range(Y):
+            joined = None
+            for i in range(ns):
+                origin = lax.rem(si - i + ns, ns)
+                moved = pltpu.roll(inb[i, c], lax.rem((origin - y + ns) * X, 128), 1)
+                here = (zlane // X) == origin
+                joined = moved if joined is None else jnp.where(here, moved, joined)
+            pieces[y] = joined
+        for b in range(Y // 4):
+            v0, v1, v2, v3 = pieces[4 * b:4 * b + 4]
+            s03, s12, d03, d12 = v0 + v3, v1 + v2, v0 - v3, v1 - v2
+            for k, value in enumerate((0.5 * (s03 + s12), c1t * d03 + c3t * d12,
+                                       0.5 * (s03 - s12), c3t * d03 - c1t * d12)):
+                coef_ref[c, 4 * b + k] = value
+        block = coef_ref[c].reshape(Y * zrows, 128)
+        done = jnp.dot(block, gt_ref[...], precision=lax.Precision.HIGHEST, preferred_element_type=jnp.float32)
+        coef_ref[c] = done.reshape(Y, zrows, 128)
+        return 0
+
+    lax.fori_loop(0, 6, gather_back, 0)
+    drain(0)
+    drain(1)
+    for i in range(1, ns):
+        trades[i].wait_send()
+
+
+def fused(mesh, u_now, u_prev, force, stiffness, broken, flags):
+    ns, ng = mesh.shape["slab"], mesh.shape["grp"]
+    _, X, Y, Z = u_now.shape
+    xe, pairs, half = X + 2 * HALO, X // 2 + HALO, X // 2
+    zrows = Z // ns
+    ez = jnp.asarray(np.kron(np.eye(Z // 4), np.ones((1, 4))), jnp.float32)
+    cz = jnp.asarray(np.kron(np.eye(Z // 4), cosine_table()), jnp.float32)
+    gt = jnp.asarray(wavelet_table(X * ns).T, jnp.float32)
+
+    def vm(*shape):
+        return pltpu.VMEM(shape, jnp.float32)
+
+    def ext(n):
+        return vm(n, xe, Y, Z)
+
+    def stage(n):
+        return vm(2, n, half, Y, Z)
+
+    def land(n):
+        return vm(2, n, pairs, Y, Z)
+
+    dma = pltpu.SemaphoreType.DMA
+    return pl.pallas_call(
+        lambda *refs: kernel(ns, ng, *refs),
+        name="lattice",
+        out_shape=(jax.ShapeDtypeStruct(u_now.shape, jnp.float32),
+                   jax.ShapeDtypeStruct((6, Y, zrows, X * ns), jnp.float32)),
+        in_specs=[pl.BlockSpec(memory_space=pltpu.VMEM)] * 9,
+        out_specs=(pl.BlockSpec(memory_space=pltpu.VMEM),) * 2,
+        scratch_shapes=[
+            ext(7), ext(7), stage(7), land(7),
+            ext(3), ext(3), stage(3), land(3),
+            ext(6), ext(6), ext(6), stage(6), land(6),
+            ext(3), ext(3), vm(X, Y, Z), ext(3), ext(3), ext(5), ext(5),
+            vm(2, ns * ng, 1, 128), vm(6, Y * X, Z), vm(ns, 6, zrows, 128), vm(ns, 6, zrows, 128),
+            dma((8,)), dma((8,)), dma((8,)), dma((8,)), dma((8,)), dma((8,)),
+            dma((2,)), dma((2,)), dma((ns,)), dma((ns,)),
+        ],
+        compiler_params=pltpu.CompilerParams(collective_id=0, has_side_effects=True, vmem_limit_bytes=48 << 20),
+    )(u_now, u_prev, force, stiffness, broken, flags, ez, cz, gt)
+
+
+def fits(mesh, shape):
+    ns, ng = mesh.shape["slab"], mesh.shape["grp"]
+    x, y, z = shape[1] // ns, shape[2] // ng, shape[3]
+    return y == 8 and z == 128 and x * y == 128 and x * ns == 128 and z % (8 * ns) == 0
+
+
+def entry(mesh, *args):
+    ns, ng = mesh.shape["slab"], mesh.shape["grp"]
+    _, x, y, z = args[0].shape
+    if fits(mesh, (3, x * ns, y * ng, z)):
+        return fused(mesh, *args)
+    return body(*args)
+
+
 def solution(mesh):
     return jax.shard_map(
-        body,
+        lambda *args: entry(mesh, *args),
         mesh=mesh,
         in_specs=(
             P(None, "slab", "grp", None),

time: 377 us -> 65 us (0.17)
  blocking collectives: 168 us -> 0 us
  starting transfers between devices: 80.6 us -> 0 us
  Pallas kernels: 0 us -> 55.1 us
  waiting for transfers between devices: 50.9 us -> 0 us
  local copies, waits for them, and re-layouts: 43.8 us -> 8.8 us
  other arithmetic: 13.9 us -> 0 us
  between operations: 13.3 us -> 0.66 us
    psum x4 -> x0, blocking collectives: 168 us -> none  [paired_sum(): lax.psum((jnp.sum(residual * residual), jnp.sum(residual * image)), ('sla...]
    ppermute x32 -> x0, starting transfers between devices: 75.1 us -> none  [the longest x16 54.2 us: with_halo(): lax.ppermute(lax.slice_in_dim(block, block.shape[dim] - width, None, axis...]
    pallas_call x0 -> x1, Pallas kernels: none -> 55.1 us  [fused(): pl.pallas_call(lambda *refs: kernel(ns, ng, *refs), name='lattice', out_s...]
    ppermute x32 -> x0, waiting for transfers between devices: 41.3 us -> none  [the longest x16 40.8 us: with_halo(): lax.ppermute(lax.slice_in_dim(block, 0, width, axis=dim), axis, backward)]
    slice x20 -> x0, local copies, waits for them, and re-layouts: 26.7 us -> none  [the longest x3 12.9 us: lift(): odd = signal[..., 1::2]]
    all_to_all x1 -> x0, waiting for transfers between devices: 9.58 us -> none  [body(): lax.all_to_all(moved, 'slab', split_axis=2, concat_axis=3, tiled=True)]
    all_to_all x3 -> x0, local copies, waits for them, and re-layouts: 6.37 us -> none  [body(): lax.all_to_all(moved, 'slab', split_axis=2, concat_axis=3, tiled=True)]
    all_to_all x1 -> x0, starting transfers between devices: 5.51 us -> none  [body(): lax.all_to_all(moved, 'slab', split_axis=2, concat_axis=3, tiled=True)]
  transfers between devices with their start and end apart: 33 -> 0, of which waited for: 19 -> 0; matrix products, arithmetic and copies ran while one was open for 1% -> 0% of each run, Pallas kernels for 0% -> 0%
where the time goes in v1:
time: 65 us; the launch traced here: 64.6 us
  Pallas kernels  55.1 us (85%)
  local copies, waits for them, and re-layouts  8.8 us (14%)
  between operations  0.66 us (1%)
    pallas_call x1, Pallas kernels, fused(): pl.pallas_call(lambda *refs: kernel(ns, ng, *refs), name='lattice', out_s...  55.1 us
    unnamed x20, local copies, waits for them, and re-layouts  8.8 us

profile of v1, /device:TPU:0, one launch (start us, length us, event | category | flops | bytes accessed | tf_op | source)
XLA Modules:
  0.0 64.6 jit_solution(14015513531338772937)
XLA Ops:
  0.6 0.0 copy-start
  0.6 0.9 %copy-done = f32[3,16,8,128]{3,2,1,0:T(8,128)S(1)} copy-done((f32[3,16,8,128]{3,2,1,0:T(8,128)S(1)}, f32[3,16,8,128]{3,2,1,0:T(8,128)}, u32[]{:S(2)}) %copy-start) | copy-done | bytes 196632
  1.6 0.0 copy-start.1
  1.6 0.9 %copy-done.1 = f32[3,16,8,128]{3,2,1,0:T(8,128)S(1)} copy-done((f32[3,16,8,128]{3,2,1,0:T(8,128)S(1)}, f32[3,16,8,128]{3,2,1,0:T(8,128)}, u32[]{:S(2)}) %copy-start.1) | copy-done | bytes 196632
  2.5 0.0 copy-start.2
  2.5 0.9 %copy-done.2 = f32[3,16,8,128]{3,2,1,0:T(8,128)S(1)} copy-done((f32[3,16,8,128]{3,2,1,0:T(8,128)S(1)}, f32[3,16,8,128]{3,2,1,0:T(8,128)}, u32[]{:S(2)}) %copy-start.2) | copy-done | bytes 196632
  3.4 0.0 copy-start.3
  3.4 0.8 %copy-done.3 = f32[16,8,128]{2,1,0:T(8,128)S(1)} copy-done((f32[16,8,128]{2,1,0:T(8,128)S(1)}, f32[16,8,128]{2,1,0:T(8,128)}, u32[]{:S(2)}) %copy-start.3) | copy-done | bytes 65560
  4.3 0.0 copy-start.4
  4.3 0.8 %copy-done.4 = f32[128,128]{1,0:T(8,128)S(1)} copy-done((f32[128,128]{1,0:T(8,128)S(1)}, f32[128,128]{1,0:T(8,128)}, u32[]{:S(2)}) %copy-start.4) | copy-done | bytes 65560
  5.1 0.0 copy-start.5
  5.1 0.8 %copy-done.5 = f32[128,128]{1,0:T(8,128)S(1)} copy-done((f32[128,128]{1,0:T(8,128)S(1)}, f32[128,128]{1,0:T(8,128)}, u32[]{:S(2)}) %copy-start.5) | copy-done | bytes 65560
  5.9 0.0 copy-start.6
  5.9 0.7 %copy-done.6 = f32[32,128]{1,0:T(8,128)S(1)} copy-done((f32[32,128]{1,0:T(8,128)S(1)}, f32[32,128]{1,0:T(8,128)}, u32[]{:S(2)}) %copy-start.6) | copy-done | bytes 16408
  6.7 0.0 copy-start.7
  6.7 0.7 %copy-done.7 = s32[4,2,32]{2,1,0:T(2,128)S(1)} copy-done((s32[4,2,32]{2,1,0:T(2,128)S(1)}, s32[4,2,32]{2,1,0:T(2,128)}, u32[]{:S(2)}) %copy-start.7) | copy-done | bytes 1048
  7.3 0.0 copy-start.8
  7.3 0.7 %copy-done.8 = s32[4,2,32]{2,1,0:T(2,128)S(1)} copy-done((s32[4,2,32]{2,1,0:T(2,128)S(1)}, s32[4,2,32]{2,1,0:T(2,128)}, u32[]{:S(2)}) %copy-start.8) | copy-done | bytes 1048
  8.0 55.1 %lattice.1 = (f32[3,16,8,128]{3,2,1,0:T(8,128)S(1)}, f32[6,8,16,128]{3,2,1,0:T(8,128)S(1)}) custom-call(f32[3,16,8,128]{3,2,1,0:T(8,128)S(1)} %copy-done, f32[3,16,8,128]{3,2,1,0:T(8,128)S(1)} %copy-done.1, f32[3,16,8,128]{3,2,1,0:T(8,128)S(1)} %copy-done.2, f32[16,8,128]{2,1,0:T(8,128)S(1)} %copy-done.3, s32[4,2,32]{2,1,0:T(2,128)S(1)} %copy-done.7, ...), custom_call_target="tpu_custom_call" | custom-call | tf_op jit(solution)/shard_map/lattice/pallas_call | solution.py:653
  63.2 0.7 %copy.13 = f32[3,16,8,128]{3,2,1,0:T(8,128)} copy(f32[3,16,8,128]{3,2,1,0:T(8,128)S(1)} %get-tuple-element.4) | data formatting | bytes 393216
  63.9 0.7 %copy.14 = f32[6,8,16,128]{3,2,1,0:T(8,128)} copy(f32[6,8,16,128]{3,2,1,0:T(8,128)S(1)} %get-tuple-element.5) | data formatting | bytes 786432
Async XLA Ops:
  0.6 0.9 %copy-start = (f32[3,16,8,128]{3,2,1,0:T(8,128)S(1)}, f32[3,16,8,128]{3,2,1,0:T(8,128)}, u32[]{:S(2)}) copy-start(f32[3,16,8,128]{3,2,1,0:T(8,128)} %refs_0_.1) | copy-start | bytes 589828
  1.6 0.9 %copy-start.1 = (f32[3,16,8,128]{3,2,1,0:T(8,128)S(1)}, f32[3,16,8,128]{3,2,1,0:T(8,128)}, u32[]{:S(2)}) copy-start(f32[3,16,8,128]{3,2,1,0:T(8,128)} %refs_1_.1) | copy-start | bytes 589828
  2.5 0.9 %copy-start.2 = (f32[3,16,8,128]{3,2,1,0:T(8,128)S(1)}, f32[3,16,8,128]{3,2,1,0:T(8,128)}, u32[]{:S(2)}) copy-start(f32[3,16,8,128]{3,2,1,0:T(8,128)} %refs_2_.1) | copy-start | bytes 589828
  3.4 0.8 %copy-start.3 = (f32[16,8,128]{2,1,0:T(8,128)S(1)}, f32[16,8,128]{2,1,0:T(8,128)}, u32[]{:S(2)}) copy-start(f32[16,8,128]{2,1,0:T(8,128)} %refs_3_.1) | copy-start | bytes 196612
  4.3 0.8 %copy-start.4 = (f32[128,128]{1,0:T(8,128)S(1)}, f32[128,128]{1,0:T(8,128)}, u32[]{:S(2)}) copy-start(f32[128,128]{1,0:T(8,128)} %constant.8.clone.refs_8_) | copy-start | bytes 196612
  5.1 0.8 %copy-start.5 = (f32[128,128]{1,0:T(8,128)S(1)}, f32[128,128]{1,0:T(8,128)}, u32[]{:S(2)}) copy-start(f32[128,128]{1,0:T(8,128)} %constant.7.clone.refs_7_) | copy-start | bytes 196612
  5.9 0.7 %copy-start.6 = (f32[32,128]{1,0:T(8,128)S(1)}, f32[32,128]{1,0:T(8,128)}, u32[]{:S(2)}) copy-start(f32[32,128]{1,0:T(8,128)} %constant.6.clone.refs_6_) | copy-start | bytes 49156
  6.7 0.7 %copy-start.7 = (s32[4,2,32]{2,1,0:T(2,128)S(1)}, s32[4,2,32]{2,1,0:T(2,128)}, u32[]{:S(2)}) copy-start(s32[4,2,32]{2,1,0:T(2,128)} %refs_4_.1) | copy-start | bytes 3076
  7.3 0.7 %copy-start.8 = (s32[4,2,32]{2,1,0:T(2,128)S(1)}, s32[4,2,32]{2,1,0:T(2,128)}, u32[]{:S(2)}) copy-start(s32[4,2,32]{2,1,0:T(2,128)} %refs_5_.1) | copy-start | bytes 3076

commit v2 on v1

--- a/solution.py
+++ b/solution.py
@@ -172,6 +172,11 @@
     return np.concatenate([approx] + pieces, axis=0)
 
 
+def split_table(table):
+    high = table.astype(jnp.bfloat16).astype(np.float64)
+    return high, (table - high).astype(jnp.bfloat16).astype(np.float64)
+
+
 def sub_index():
     return lax.broadcasted_iota(jnp.int32, (8, 128), 0)
 
@@ -204,8 +209,9 @@
     return jnp.sum(jnp.sum(v, axis=0, keepdims=True), axis=1, keepdims=True)
 
 
-def kernel(ns, ng, u_ref, p_ref, f_ref, k_ref, br_ref, fl_ref, ez_ref, cz_ref, gt_ref,
+def kernel(ns, ng, u_in, p_in, f_in, k_in, br_in, fl_in, ez_in, cz_in, gt_in,
            disp_ref, coef_ref,
+           u_ref, p_ref, f_ref, k_ref, br_ref, fl_ref, ez_ref, cz_ref, gt_ref, isem,
            e1a, e1b, s1, h1, e2a, e2b, s2, h2, rqa, rqb, e3a, s3, h3,
            u1a, u1b, carry, dga, dgb, kca, kcb, gath, rows, outb, inb,
            send1, recv1, send2, recv2, send3, recv3, asend, arecv, tsend, trecv):
@@ -213,6 +219,14 @@
     si, gi = lax.axis_index("slab"), lax.axis_index("grp")
     me = si * ng + gi
     count = ns * ng
+    fetched = []
+    for at, (source, target) in enumerate((
+        (br_in, br_ref), (fl_in, fl_ref), (ez_in, ez_ref), (k_in, k_ref), (u_in, u_ref), (p_in, p_ref),
+        (f_in, f_ref), (cz_in, cz_ref), (gt_in, gt_ref),
+    )):
+        fetch = pltpu.make_async_copy(source, target, isem.at[at])
+        fetch.start()
+        fetched.append(fetch)
     barrier = pltpu.get_barrier_semaphore()
 
     def greet(i, _):
@@ -318,6 +332,8 @@
         wide = jnp.dot(mask.astype(jnp.float32), ez_ref[...], preferred_element_type=jnp.float32)
         return jnp.where(upper, jnp.broadcast_to(wide[0:1], (8, 128)), jnp.broadcast_to(wide[1:2], (8, 128)))
 
+    for at in range(4):
+        fetched[at].wait()
     for bx in range(X // 4):
         cut = 1.0 - CRACK_CUT * spread_rows(br_ref[bx])
         flag = spread_rows(fl_ref[bx])
@@ -345,6 +361,8 @@
         pack(s1, 6, i, e1a[6, HALO + 2 * i], e1a[6, HALO + 2 * i + 1])
         return 0
 
+    for at in range(4, 7):
+        fetched[at].wait()
     lax.fori_loop(0, X // 2, own, 0)
     blank(e1a, h1)
     blank(e2a, h2)
@@ -398,7 +416,7 @@
     kcb[0, HALO - REACH] = link(e1b[6, HALO - REACH], e1b[6, HALO - REACH + 1])
     lax.fori_loop(HALO - 2, HALO + X + 2, coefficients, 0)
 
-    def operate(x, va, vb, base):
+    def operate(x, va, vb, base, both=True):
         result = []
         coef = [[kc[j, x] for j in range(5)] + [kc[0, x - 1]] for kc in (kca, kcb)]
         for c in range(3):
@@ -406,7 +424,8 @@
             ua, ub = up_y(a, b)
             la, lb = down_y(a, b)
             pair = []
-            for v, ref, u, l, k, dg in ((a, va, ua, la, coef[0], dga), (b, vb, ub, lb, coef[1], dgb)):
+            halves = ((a, va, ua, la, coef[0], dga), (b, vb, ub, lb, coef[1], dgb))
+            for v, ref, u, l, k, dg in halves if both else halves[:1]:
                 parts = (
                     k[0] * ref[base + c, x + 1] + k[5] * ref[base + c, x - 1],
                     k[1] * u + k[2] * l,
@@ -418,47 +437,56 @@
         return result
 
     def solve(step, va, vb, rhs_of):
-        def residual(x, _):
-            image = operate(x, va, vb, 0)
-            for c in range(3):
-                ra, rb = rhs_of(c, x)
-                rqa[c, x] = ra - image[c][0]
-                rqb[c, x] = rb - image[c][1]
+        def residual(i, _):
+            done = []
+            for x in (2 * i, 2 * i + 1):
+                image = operate(x, va, vb, 0)
+                for c in range(3):
+                    ra, rb = rhs_of(c, x)
+                    done.append((c, x, ra - image[c][0], rb - image[c][1]))
+            for c, x, ra, rb in done:
+                rqa[c, x] = ra
+                rqb[c, x] = rb
             return 0
 
-        lax.fori_loop(HALO - 2, HALO + X + 2, residual, 0)
-
-        def apply(x, _):
-            image = operate(x, rqa, rqb, 0)
+        lax.fori_loop((HALO - 2) // 2, (HALO + X + 2) // 2, residual, 0)
+
+        def put(x, image):
             for c in range(3):
                 rqa[3 + c, x] = image[c][0]
                 rqb[3 + c, x] = image[c][1]
-            return 0
-
-        lax.fori_loop(HALO - 1, HALO + X + 1, apply, 0)
-
-        def products(x, sums):
+
+        def apply(i, sums):
             rr, rq = sums
-            for c in range(3):
-                r, q = rqa[c, x], rqa[3 + c, x]
-                rr, rq = rr + r * r, rq + r * q
+            at = (2 * i, 2 * i + 1)
+            images = [operate(x, rqa, rqb, 0) for x in at]
+            for x, image in zip(at, images):
+                for c in range(3):
+                    r = rqa[c, x]
+                    rr, rq = rr + r * r, rq + r * image[c][0]
+            for x, image in zip(at, images):
+                put(x, image)
             return rr, rq
 
         zero = jnp.zeros((8, 128), jnp.float32)
-        rr, rq = lax.fori_loop(HALO, HALO + X, products, (zero, zero))
+        images = [operate(x, rqa, rqb, 0) for x in (HALO - 1, HALO + X)]
+        put(HALO - 1, images[0])
+        put(HALO + X, images[1])
+        rr, rq = lax.fori_loop(HALO // 2, (HALO + X) // 2, apply, (zero, zero))
         rr, rq = total(rr), total(rq)
         mu = jnp.where(rr > 0.0, rq / jnp.where(rr > 0.0, rr, 1.0), 0.0)
 
-        def centred(x, sums):
+        def centred(i, sums):
             ww, wr, mix, wt = sums
-            image = operate(x, rqa, rqb, 3)
-            for c in range(3):
-                r, q, s = rqa[c, x], rqa[3 + c, x], image[c][0]
-                w, t = q - mu * r, s - mu * q
-                ww, wr, mix, wt = ww + w * w, wr + w * r, mix + (r * t + w * q), wt + w * t
+            for x in (2 * i, 2 * i + 1):
+                image = operate(x, rqa, rqb, 3, False)
+                for c in range(3):
+                    r, q, s = rqa[c, x], rqa[3 + c, x], image[c][0]
+                    w, t = q - mu * r, s - mu * q
+                    ww, wr, mix, wt = ww + w * w, wr + w * r, mix + (r * t + w * q), wt + w * t
             return ww, wr, mix, wt
 
-        sums = lax.fori_loop(HALO, HALO + X, centred, (zero,) * 4)
+        sums = lax.fori_loop(HALO // 2, (HALO + X) // 2, centred, (zero,) * 4)
         ww, wr, mix, wt = [total(v) for v in sums]
         one = lax.broadcasted_iota(jnp.int32, (1, 128), 1)
         row = jnp.zeros((1, 128), jnp.float32)
@@ -556,76 +584,105 @@
             u1b[c, x] = vb
         return 0
 
-    lax.fori_loop(HALO - 1, HALO + X + 1, step2, 0)
-
-    def finals(x, _):
-        at = x - HALO
-        scale = SPRING_NORMAL * carry[at] * 0.5
-        values = [u1a[c, x] for c in range(3)]
-        for c in range(3):
-            disp_ref[c, at] = values[c]
-        dx = u1a[0, x + 1] - u1a[0, x - 1]
-        dy = up_y(values[1], u1b[1, x])[0] - down_y(values[1], u1b[1, x])[0]
-        dz = jnp.where(not_last, up_z(values[2]), 0.0) - jnp.where(not_first, down_z(values[2]), 0.0)
-        for c, v in enumerate(values + [scale * dx, scale * dy, scale * dz]):
-            rows[c, pl.ds(at, 8, stride=X), :] = v
-        return 0
-
-    lax.fori_loop(HALO, HALO + X, finals, 0)
-
+    step2(HALO - 1, 0)
+    step2(HALO + X, 0)
+
+    def step2_own(i, _):
+        for x in (2 * i, 2 * i + 1):
+            step2(x, 0)
+            for c in range(3):
+                v = u1a[c, x]
+                disp_ref[c, x - HALO] = v
+                rows[c, pl.ds(x - HALO, 8, stride=X), :] = v
+        return 0
+
+    lax.fori_loop(HALO // 2, (HALO + X) // 2, step2_own, 0)
     zrows = coef_ref.shape[2]
+    nt = (((1,), (1,)), ((), ()))
+
+    def halves(v):
+        high = v.astype(jnp.bfloat16)
+        return high, (v - high.astype(jnp.float32)).astype(jnp.bfloat16)
 
     def transform(c, _):
-        turned = lax.dot_general(cz_ref[...], rows[c], (((1,), (1,)), ((), ())),
-                                 precision=lax.Precision.HIGHEST, preferred_element_type=jnp.float32)
+        high, low = halves(rows[c])
+        turned = lax.dot_general(cz_ref[:, 0:256], jnp.concatenate([high, low], axis=1), nt,
+                                 preferred_element_type=jnp.float32)
+        turned += lax.dot_general(cz_ref[:, 256:384], high, nt, preferred_element_type=jnp.float32)
         for j in range(ns):
             outb[j, c] = turned[j * zrows:(j + 1) * zrows]
         return 0
 
-    lax.fori_loop(0, 6, transform, 0)
-
-    def trade(i):
+    def trade(part, i):
         to = lax.rem(si + i, ns)
         return pltpu.make_async_remote_copy(
-            src_ref=outb.at[to], dst_ref=inb.at[i], send_sem=tsend.at[i], recv_sem=trecv.at[i],
+            src_ref=outb.at[to, pl.ds(3 * part, 3)], dst_ref=inb.at[si, pl.ds(3 * part, 3)],
+            send_sem=tsend.at[part, i], recv_sem=trecv.at[part, i],
             device_id=(to, gi), device_id_type=MESH)
 
-    trades = [None] + [trade(i) for i in range(1, ns)]
-    for i in range(1, ns):
-        trades[i].start()
-    inb[0] = outb[si]
-    for i in range(1, ns):
-        trades[i].wait_recv()
+    trades = [[trade(part, i) for i in range(1, ns)] for part in range(2)]
+
+    def ship(part):
+        lax.fori_loop(3 * part, 3 * part + 3, transform, 0)
+        for copy in trades[part]:
+            copy.start()
+        for c in range(3 * part, 3 * part + 3):
+            inb[si, c] = outb[si, c]
+
+    fetched[7].wait()
+    ship(0)
+
+    def finals(i, _):
+        for x in (2 * i, 2 * i + 1):
+            at = x - HALO
+            scale = SPRING_NORMAL * carry[at] * 0.5
+            a1, a2, b1 = u1a[1, x], u1a[2, x], u1b[1, x]
+            dx = u1a[0, x + 1] - u1a[0, x - 1]
+            dy = up_y(a1, b1)[0] - down_y(a1, b1)[0]
+            dz = jnp.where(not_last, up_z(a2), 0.0) - jnp.where(not_first, down_z(a2), 0.0)
+            for c, d in enumerate((dx, dy, dz)):
+                rows[3 + c, pl.ds(at, 8, stride=X), :] = scale * d
+        return 0
+
+    lax.fori_loop(HALO // 2, (HALO + X) // 2, finals, 0)
+    ship(1)
+    fetched[8].wait()
 
     zlane = lax.broadcasted_iota(jnp.int32, (zrows, 128), 1)
     c1t, c3t = float(np.sqrt(0.5) * np.cos(np.pi / 8)), float(np.sqrt(0.5) * np.cos(3 * np.pi / 8))
 
     def gather_back(c, _):
-        pieces = [None] * Y
-        for y in range(Y):
-            joined = None
-            for i in range(ns):
-                origin = lax.rem(si - i + ns, ns)
-                moved = pltpu.roll(inb[i, c], lax.rem((origin - y + ns) * X, 128), 1)
-                here = (zlane // X) == origin
-                joined = moved if joined is None else jnp.where(here, moved, joined)
-            pieces[y] = joined
+        pieces = [inb[j, c] for j in range(ns)]
+        gap = ns // 2
+        while gap:
+            keep = (zlane // (X * gap)) % 2 == 0
+            mixed = list(pieces)
+            for j in range(ns):
+                if (j // gap) % 2 == 0:
+                    a, b = pieces[j], pieces[j + gap]
+                    mixed[j] = jnp.where(keep, a, pltpu.roll(b, X * gap, 1))
+                    mixed[j + gap] = jnp.where(keep, pltpu.roll(a, 128 - X * gap, 1), b)
+            pieces = mixed
+            gap //= 2
+        coded = []
         for b in range(Y // 4):
             v0, v1, v2, v3 = pieces[4 * b:4 * b + 4]
             s03, s12, d03, d12 = v0 + v3, v1 + v2, v0 - v3, v1 - v2
-            for k, value in enumerate((0.5 * (s03 + s12), c1t * d03 + c3t * d12,
-                                       0.5 * (s03 - s12), c3t * d03 - c1t * d12)):
-                coef_ref[c, 4 * b + k] = value
-        block = coef_ref[c].reshape(Y * zrows, 128)
-        done = jnp.dot(block, gt_ref[...], precision=lax.Precision.HIGHEST, preferred_element_type=jnp.float32)
-        coef_ref[c] = done.reshape(Y, zrows, 128)
-        return 0
-
-    lax.fori_loop(0, 6, gather_back, 0)
+            coded += [0.5 * (s03 + s12), c1t * d03 + c3t * d12, 0.5 * (s03 - s12), c3t * d03 - c1t * d12]
+        high, low = halves(jnp.concatenate(coded, axis=0))
+        done = jnp.dot(jnp.concatenate([high, low], axis=1), gt_ref[...], preferred_element_type=jnp.float32)
+        coef_ref[c] = (done[:, 0:128] + done[:, 128:256]).reshape(Y, zrows, 128)
+        return 0
+
+    for part in range(2):
+        for copy in trades[part]:
+            copy.wait_recv()
+        lax.fori_loop(3 * part, 3 * part + 3, gather_back, 0)
     drain(0)
     drain(1)
-    for i in range(1, ns):
-        trades[i].wait_send()
+    for part in range(2):
+        for copy in trades[part]:
+            copy.wait_send()
 
 
 def fused(mesh, u_now, u_prev, force, stiffness, broken, flags):
@@ -634,8 +691,10 @@
     xe, pairs, half = X + 2 * HALO, X // 2 + HALO, X // 2
     zrows = Z // ns
     ez = jnp.asarray(np.kron(np.eye(Z // 4), np.ones((1, 4))), jnp.float32)
-    cz = jnp.asarray(np.kron(np.eye(Z // 4), cosine_table()), jnp.float32)
-    gt = jnp.asarray(wavelet_table(X * ns).T, jnp.float32)
+    czh, czl = split_table(np.kron(np.eye(Z // 4), cosine_table()))
+    cz = jnp.asarray(np.concatenate([czh, czh, czl], axis=1), jnp.bfloat16)
+    gth, gtl = split_table(wavelet_table(X * ns).T)
+    gt = jnp.asarray(np.block([[gth, gtl], [gth, np.zeros_like(gtl)]]), jnp.bfloat16)
 
     def vm(*shape):
         return pltpu.VMEM(shape, jnp.float32)
@@ -655,16 +714,19 @@
         name="lattice",
         out_shape=(jax.ShapeDtypeStruct(u_now.shape, jnp.float32),
                    jax.ShapeDtypeStruct((6, Y, zrows, X * ns), jnp.float32)),
-        in_specs=[pl.BlockSpec(memory_space=pltpu.VMEM)] * 9,
+        in_specs=[pl.BlockSpec(memory_space=pltpu.MemorySpace.HBM)] * 9,
         out_specs=(pl.BlockSpec(memory_space=pltpu.VMEM),) * 2,
         scratch_shapes=[
+            vm(*u_now.shape), vm(*u_now.shape), vm(*u_now.shape), vm(*stiffness.shape),
+            pltpu.VMEM(broken.shape, broken.dtype), pltpu.VMEM(flags.shape, flags.dtype),
+            vm(*ez.shape), pltpu.VMEM(cz.shape, cz.dtype), pltpu.VMEM(gt.shape, gt.dtype), pltpu.SemaphoreType.DMA((9,)),
             ext(7), ext(7), stage(7), land(7),
             ext(3), ext(3), stage(3), land(3),
             ext(6), ext(6), ext(6), stage(6), land(6),
             ext(3), ext(3), vm(X, Y, Z), ext(3), ext(3), ext(5), ext(5),
             vm(2, ns * ng, 1, 128), vm(6, Y * X, Z), vm(ns, 6, zrows, 128), vm(ns, 6, zrows, 128),
             dma((8,)), dma((8,)), dma((8,)), dma((8,)), dma((8,)), dma((8,)),
-            dma((2,)), dma((2,)), dma((ns,)), dma((ns,)),
+            dma((2,)), dma((2,)), dma((2, ns)), dma((2, ns)),
         ],
         compiler_params=pltpu.CompilerParams(collective_id=0, has_side_effects=True, vmem_limit_bytes=48 << 20),
     )(u_now, u_prev, force, stiffness, broken, flags, ez, cz, gt)

time: 65 us -> 59.8 us (0.920)
  Pallas kernels: 55.1 us -> 49.8 us
    pallas_call x1, Pallas kernels: 55.1 us -> 49.8 us  [fused(): pl.pallas_call(lambda *refs: kernel(ns, ng, *refs), name='lattice', out_s...]
where the time goes in v2:
time: 59.8 us; the launch traced here: 59.4 us
  Pallas kernels  49.8 us (83%)
  local copies, waits for them, and re-layouts  8.92 us (15%)
  between operations  0.66 us (1%)
    pallas_call x1, Pallas kernels, fused(): pl.pallas_call(lambda *refs: kernel(ns, ng, *refs), name='lattice', out_s...  49.8 us
    unnamed x20, local copies, waits for them, and re-layouts  8.92 us

profile of v2, /device:TPU:0, one launch (start us, length us, event | category | flops | bytes accessed | tf_op | source)
XLA Modules:
  0.0 59.4 jit_solution(5371462588115360473)
XLA Ops:
  0.6 0.0 copy-start
  0.6 0.9 %copy-done = f32[3,16,8,128]{3,2,1,0:T(8,128)S(1)} copy-done((f32[3,16,8,128]{3,2,1,0:T(8,128)S(1)}, f32[3,16,8,128]{3,2,1,0:T(8,128)}, u32[]{:S(2)}) %copy-start) | copy-done | bytes 196632
  1.6 0.0 copy-start.1
  1.6 0.9 %copy-done.1 = f32[3,16,8,128]{3,2,1,0:T(8,128)S(1)} copy-done((f32[3,16,8,128]{3,2,1,0:T(8,128)S(1)}, f32[3,16,8,128]{3,2,1,0:T(8,128)}, u32[]{:S(2)}) %copy-start.1) | copy-done | bytes 196632
  2.5 0.0 copy-start.2
  2.5 0.9 %copy-done.2 = f32[3,16,8,128]{3,2,1,0:T(8,128)S(1)} copy-done((f32[3,16,8,128]{3,2,1,0:T(8,128)S(1)}, f32[3,16,8,128]{3,2,1,0:T(8,128)}, u32[]{:S(2)}) %copy-start.2) | copy-done | bytes 196632
  3.4 0.0 copy-start.3
  3.4 0.9 %copy-done.3 = bf16[256,256]{1,0:T(8,128)(2,1)S(1)} copy-done((bf16[256,256]{1,0:T(8,128)(2,1)S(1)}, bf16[256,256]{1,0:T(8,128)(2,1)}, u32[]{:S(2)}) %copy-start.3) | copy-done | bytes 131096
  4.3 0.0 copy-start.4
  4.3 0.9 %copy-done.4 = bf16[128,384]{1,0:T(8,128)(2,1)S(1)} copy-done((bf16[128,384]{1,0:T(8,128)(2,1)S(1)}, bf16[128,384]{1,0:T(8,128)(2,1)}, u32[]{:S(2)}) %copy-start.4) | copy-done | bytes 98328
  5.2 0.0 copy-start.5
  5.2 0.8 %copy-done.5 = f32[16,8,128]{2,1,0:T(8,128)S(1)} copy-done((f32[16,8,128]{2,1,0:T(8,128)S(1)}, f32[16,8,128]{2,1,0:T(8,128)}, u32[]{:S(2)}) %copy-start.5) | copy-done | bytes 65560
  6.1 0.0 copy-start.6
  6.1 0.7 %copy-done.6 = f32[32,128]{1,0:T(8,128)S(1)} copy-done((f32[32,128]{1,0:T(8,128)S(1)}, f32[32,128]{1,0:T(8,128)}, u32[]{:S(2)}) %copy-start.6) | copy-done | bytes 16408
  6.8 0.0 copy-start.7
  6.8 0.7 %copy-done.7 = s32[4,2,32]{2,1,0:T(2,128)S(1)} copy-done((s32[4,2,32]{2,1,0:T(2,128)S(1)}, s32[4,2,32]{2,1,0:T(2,128)}, u32[]{:S(2)}) %copy-start.7) | copy-done | bytes 1048
  7.5 0.0 copy-start.8
  7.5 0.7 %copy-done.8 = s32[4,2,32]{2,1,0:T(2,128)S(1)} copy-done((s32[4,2,32]{2,1,0:T(2,128)S(1)}, s32[4,2,32]{2,1,0:T(2,128)}, u32[]{:S(2)}) %copy-start.8) | copy-done | bytes 1048
  8.1 49.8 %lattice.1 = (f32[3,16,8,128]{3,2,1,0:T(8,128)S(1)}, f32[6,8,16,128]{3,2,1,0:T(8,128)S(1)}) custom-call(f32[3,16,8,128]{3,2,1,0:T(8,128)S(1)} %copy-done, f32[3,16,8,128]{3,2,1,0:T(8,128)S(1)} %copy-done.1, f32[3,16,8,128]{3,2,1,0:T(8,128)S(1)} %copy-done.2, f32[16,8,128]{2,1,0:T(8,128)S(1)} %copy-done.5, s32[4,2,32]{2,1,0:T(2,128)S(1)} %copy-done.7, ...), custom_call_target="tpu_custom_call" | custom-call | tf_op jit(solution)/shard_map/lattice/pallas_call | solution.py:712
  58.0 0.7 %copy.13 = f32[3,16,8,128]{3,2,1,0:T(8,128)} copy(f32[3,16,8,128]{3,2,1,0:T(8,128)S(1)} %get-tuple-element.4) | data formatting | bytes 393216
  58.7 0.7 %copy.14 = f32[6,8,16,128]{3,2,1,0:T(8,128)} copy(f32[6,8,16,128]{3,2,1,0:T(8,128)S(1)} %get-tuple-element.5) | data formatting | bytes 786432
Async XLA Ops:
  0.6 0.9 %copy-start = (f32[3,16,8,128]{3,2,1,0:T(8,128)S(1)}, f32[3,16,8,128]{3,2,1,0:T(8,128)}, u32[]{:S(2)}) copy-start(f32[3,16,8,128]{3,2,1,0:T(8,128)} %refs_0_.1) | copy-start | bytes 589828
  1.6 0.9 %copy-start.1 = (f32[3,16,8,128]{3,2,1,0:T(8,128)S(1)}, f32[3,16,8,128]{3,2,1,0:T(8,128)}, u32[]{:S(2)}) copy-start(f32[3,16,8,128]{3,2,1,0:T(8,128)} %refs_1_.1) | copy-start | bytes 589828
  2.5 0.9 %copy-start.2 = (f32[3,16,8,128]{3,2,1,0:T(8,128)S(1)}, f32[3,16,8,128]{3,2,1,0:T(8,128)}, u32[]{:S(2)}) copy-start(f32[3,16,8,128]{3,2,1,0:T(8,128)} %refs_2_.1) | copy-start | bytes 589828
  3.4 0.9 %copy-start.3 = (bf16[256,256]{1,0:T(8,128)(2,1)S(1)}, bf16[256,256]{1,0:T(8,128)(2,1)}, u32[]{:S(2)}) copy-start(bf16[256,256]{1,0:T(8,128)(2,1)} %constant.8.clone.refs_8_) | copy-start | bytes 393220
  4.3 0.9 %copy-start.4 = (bf16[128,384]{1,0:T(8,128)(2,1)S(1)}, bf16[128,384]{1,0:T(8,128)(2,1)}, u32[]{:S(2)}) copy-start(bf16[128,384]{1,0:T(8,128)(2,1)} %constant.7.clone.refs_7_) | copy-start | bytes 294916
  5.2 0.8 %copy-start.5 = (f32[16,8,128]{2,1,0:T(8,128)S(1)}, f32[16,8,128]{2,1,0:T(8,128)}, u32[]{:S(2)}) copy-start(f32[16,8,128]{2,1,0:T(8,128)} %refs_3_.1) | copy-start | bytes 196612
  6.1 0.7 %copy-start.6 = (f32[32,128]{1,0:T(8,128)S(1)}, f32[32,128]{1,0:T(8,128)}, u32[]{:S(2)}) copy-start(f32[32,128]{1,0:T(8,128)} %constant.6.clone.refs_6_) | copy-start | bytes 49156
  6.8 0.7 %copy-start.7 = (s32[4,2,32]{2,1,0:T(2,128)S(1)}, s32[4,2,32]{2,1,0:T(2,128)}, u32[]{:S(2)}) copy-start(s32[4,2,32]{2,1,0:T(2,128)} %refs_4_.1) | copy-start | bytes 3076
  7.5 0.7 %copy-start.8 = (s32[4,2,32]{2,1,0:T(2,128)S(1)}, s32[4,2,32]{2,1,0:T(2,128)}, u32[]{:S(2)}) copy-start(s32[4,2,32]{2,1,0:T(2,128)} %refs_5_.1) | copy-start | bytes 3076

commit v3 on v2

--- a/solution.py
+++ b/solution.py
@@ -210,11 +210,11 @@
 
 
 def kernel(ns, ng, u_in, p_in, f_in, k_in, br_in, fl_in, ez_in, cz_in, gt_in,
-           disp_ref, coef_ref,
-           u_ref, p_ref, f_ref, k_ref, br_ref, fl_ref, ez_ref, cz_ref, gt_ref, isem,
+           disp_out, coef_out,
+           disp_ref, coef_ref, osem, u_ref, p_ref, f_ref, k_ref, br_ref, fl_ref, ez_ref, cz_ref, gt_ref, isem,
            e1a, e1b, s1, h1, e2a, e2b, s2, h2, rqa, rqb, e3a, s3, h3,
            u1a, u1b, carry, dga, dgb, kca, kcb, gath, rows, outb, inb,
-           send1, recv1, send2, recv2, send3, recv3, asend, arecv, tsend, trecv):
+           send0, recv0, send1, recv1, send2, recv2, send3, recv3, asend, arecv, tsend, trecv):
     X, Y = u_ref.shape[1], u_ref.shape[2]
     si, gi = lax.axis_index("slab"), lax.axis_index("grp")
     me = si * ng + gi
@@ -250,28 +250,29 @@
             ok = more if ok is None else jnp.logical_and(ok, more)
         return ok
 
-    def copies(ea, dst_a, stage, land, send, recv):
+    def copies(ea, dst_a, stage, land, send, recv, low=0, high=None):
         half = X // 2
         edge = HALO // 2
         made = []
+        chans = pl.ds(low, (ea.shape[0] if high is None else high) - low)
         for at, (ds, dg) in enumerate(steps):
             if dg == 0:
                 if ds < 0:
-                    source = ea.at[:, pl.ds(HALO, REACH)]
-                    target = dst_a.at[:, pl.ds(HALO + X, REACH)]
+                    source = ea.at[chans, pl.ds(HALO, REACH)]
+                    target = dst_a.at[chans, pl.ds(HALO + X, REACH)]
                 else:
-                    source = ea.at[:, pl.ds(HALO + X - REACH, REACH)]
-                    target = dst_a.at[:, pl.ds(HALO - REACH, REACH)]
+                    source = ea.at[chans, pl.ds(HALO + X - REACH, REACH)]
+                    target = dst_a.at[chans, pl.ds(HALO - REACH, REACH)]
             else:
                 side = 0 if dg < 0 else 1
                 if ds == 0:
-                    source, target = stage.at[side], land.at[side, :, pl.ds(edge, half)]
+                    source, target = stage.at[side, chans], land.at[side, chans, pl.ds(edge, half)]
                 elif ds < 0:
-                    source = stage.at[side, :, pl.ds(0, edge)]
-                    target = land.at[side, :, pl.ds(edge + half, edge)]
+                    source = stage.at[side, chans, pl.ds(0, 1)]
+                    target = land.at[side, chans, pl.ds(edge + half, 1)]
                 else:
-                    source = stage.at[side, :, pl.ds(half - edge, edge)]
-                    target = land.at[side, :, pl.ds(0, edge)]
+                    source = stage.at[side, chans, pl.ds(half - 1, 1)]
+                    target = land.at[side, chans, pl.ds(edge - 1, 1)]
             made.append((ds, dg, pltpu.make_async_remote_copy(
                 src_ref=source, dst_ref=target, send_sem=send.at[at], recv_sem=recv.at[at ^ 1 if at < 4 else 11 - at],
                 device_id=(si + ds, gi + dg), device_id_type=MESH)))
@@ -368,20 +369,25 @@
     blank(e2a, h2)
     blank(e3a, h3)
 
-    first = copies(e1a, e1a, s1, h1, send1, recv1)
+    zeroth = copies(e1a, e1a, s1, h1, send0, recv0, 6, 7)
+    first = copies(e1a, e1a, s1, h1, send1, recv1, 0, 6)
     second = copies(e2a, e2a, s2, h2, send2, recv2)
     third = copies(rqa, e3a, s3, h3, send3, recv3)
     pl.semaphore_wait(barrier, count - 1)
+    begin(zeroth)
     begin(first)
-    finish_recv(first, recv1)
-    begin(second)
+    finish_recv(zeroth, recv0)
+
+    def open0(i, _):
+        e1b[6, 2 * i], e1b[6, 2 * i + 1] = unpack(h1, 6, i)
+        return 0
 
     def open1(i, _):
-        for ch in range(7):
+        for ch in range(6):
             e1b[ch, 2 * i], e1b[ch, 2 * i + 1] = unpack(h1, ch, i)
         return 0
 
-    lax.fori_loop(0, (X + 2 * HALO) // 2, open1, 0)
+    lax.fori_loop(0, (X + 2 * HALO) // 2, open0, 0)
 
     def link(w, other):
         return jnp.where(jnp.minimum(w, other) > 0.0, 0.5 * (w + other), 0.0)
@@ -415,6 +421,9 @@
     kca[0, HALO - REACH] = link(e1a[6, HALO - REACH], e1a[6, HALO - REACH + 1])
     kcb[0, HALO - REACH] = link(e1b[6, HALO - REACH], e1b[6, HALO - REACH + 1])
     lax.fori_loop(HALO - 2, HALO + X + 2, coefficients, 0)
+    finish_recv(first, recv1)
+    begin(second)
+    lax.fori_loop(0, (X + 2 * HALO) // 2, open1, 0)
 
     def operate(x, va, vb, base, both=True):
         result = []
@@ -565,6 +574,7 @@
     for x in list(range(HALO - REACH, HALO)) + list(range(HALO + X, HALO + X + REACH)):
         for c in range(3):
             u1a[c, x] = e1a[c, x] + (c0 * e3a[c, x] + c1 * e3a[3 + c, x])
+    finish_send(zeroth)
     finish_send(first)
     finish_send(second)
     finish_send(third)
@@ -597,6 +607,8 @@
         return 0
 
     lax.fori_loop(HALO // 2, (HALO + X) // 2, step2_own, 0)
+    outputs = [pltpu.make_async_copy(disp_ref, disp_out, osem.at[6])]
+    outputs += [pltpu.make_async_copy(coef_ref.at[c], coef_out.at[c], osem.at[c]) for c in range(6)]
     zrows = coef_ref.shape[2]
     nt = (((1,), (1,)), ((), ()))
 
@@ -631,6 +643,7 @@
 
     fetched[7].wait()
     ship(0)
+    outputs[0].start()
 
     def finals(i, _):
         for x in (2 * i, 2 * i + 1):
@@ -677,12 +690,16 @@
     for part in range(2):
         for copy in trades[part]:
             copy.wait_recv()
-        lax.fori_loop(3 * part, 3 * part + 3, gather_back, 0)
+        for c in range(3 * part, 3 * part + 3):
+            gather_back(c, 0)
+            outputs[1 + c].start()
     drain(0)
     drain(1)
     for part in range(2):
         for copy in trades[part]:
             copy.wait_send()
+    for copy in outputs:
+        copy.wait()
 
 
 def fused(mesh, u_now, u_prev, force, stiffness, broken, flags):
@@ -715,8 +732,9 @@
         out_shape=(jax.ShapeDtypeStruct(u_now.shape, jnp.float32),
                    jax.ShapeDtypeStruct((6, Y, zrows, X * ns), jnp.float32)),
         in_specs=[pl.BlockSpec(memory_space=pltpu.MemorySpace.HBM)] * 9,
-        out_specs=(pl.BlockSpec(memory_space=pltpu.VMEM),) * 2,
+        out_specs=(pl.BlockSpec(memory_space=pltpu.MemorySpace.HBM),) * 2,
         scratch_shapes=[
+            vm(*u_now.shape), vm(6, Y, zrows, X * ns), pltpu.SemaphoreType.DMA((7,)),
             vm(*u_now.shape), vm(*u_now.shape), vm(*u_now.shape), vm(*stiffness.shape),
             pltpu.VMEM(broken.shape, broken.dtype), pltpu.VMEM(flags.shape, flags.dtype),
             vm(*ez.shape), pltpu.VMEM(cz.shape, cz.dtype), pltpu.VMEM(gt.shape, gt.dtype), pltpu.SemaphoreType.DMA((9,)),
@@ -725,10 +743,10 @@
             ext(6), ext(6), ext(6), stage(6), land(6),
             ext(3), ext(3), vm(X, Y, Z), ext(3), ext(3), ext(5), ext(5),
             vm(2, ns * ng, 1, 128), vm(6, Y * X, Z), vm(ns, 6, zrows, 128), vm(ns, 6, zrows, 128),
-            dma((8,)), dma((8,)), dma((8,)), dma((8,)), dma((8,)), dma((8,)),
+            dma((8,)), dma((8,)), dma((8,)), dma((8,)), dma((8,)), dma((8,)), dma((8,)), dma((8,)),
             dma((2,)), dma((2,)), dma((2, ns)), dma((2, ns)),
         ],
-        compiler_params=pltpu.CompilerParams(collective_id=0, has_side_effects=True, vmem_limit_bytes=48 << 20),
+        compiler_params=pltpu.CompilerParams(collective_id=0, has_side_effects=True, vmem_limit_bytes=60 << 20),
     )(u_now, u_prev, force, stiffness, broken, flags, ez, cz, gt)
 
 

time: 59.8 us -> 47.3 us (0.79)
  local copies, waits for them, and re-layouts: 8.92 us -> 2.42 us
  Pallas kernels: 49.8 us -> 44.1 us
    unnamed x20 -> x4, local copies, waits for them, and re-layouts: 8.92 us -> 2.42 us
    pallas_call x1, Pallas kernels: 49.8 us -> 44.1 us  [fused(): pl.pallas_call(lambda *refs: kernel(ns, ng, *refs), name='lattice', out_s...]
where the time goes in v3:
time: 47.3 us; the launch traced here: 47.1 us
  Pallas kernels  44.1 us (93%)
  local copies, waits for them, and re-layouts  2.42 us (5%)
  between operations  0.65 us (1%)
    pallas_call x1, Pallas kernels, fused(): pl.pallas_call(lambda *refs: kernel(ns, ng, *refs), name='lattice', out_s...  44.1 us
    unnamed x4, local copies, waits for them, and re-layouts  2.42 us

profile of v3, /device:TPU:0, one launch (start us, length us, event | category | flops | bytes accessed | tf_op | source)
XLA Modules:
  0.0 47.1 jit_solution(11979361771501463305)
XLA Ops:
  0.6 44.1 %lattice.1 = (f32[3,16,8,128]{3,2,1,0:T(8,128)}, f32[6,8,16,128]{3,2,1,0:T(8,128)}) custom-call(f32[3,16,8,128]{3,2,1,0:T(8,128)} %refs_0_.1, f32[3,16,8,128]{3,2,1,0:T(8,128)} %refs_1_.1, f32[3,16,8,128]{3,2,1,0:T(8,128)} %refs_2_.1, f32[16,8,128]{2,1,0:T(8,128)} %refs_3_.1, s32[4,2,32]{2,1,0:T(2,128)} %refs_4_.1, s32[4,2,32]{2,1,0:T(2,128)} %refs_5_.1, ...), custom_call_target="tpu_custom_call" | custom-call | tf_op jit(solution)/shard_map/lattice/pallas_call | solution.py:729
  44.7 0.0 copy-start
  44.7 1.7 %copy.13 = f32[3,16,8,128]{3,2,1,0:T(8,128)} copy(f32[3,16,8,128]{3,2,1,0:T(8,128)} %get-tuple-element.4) | data formatting | bytes 393216
  46.4 0.0 copy-done
  46.4 0.7 %copy.14 = f32[6,8,16,128]{3,2,1,0:T(8,128)} copy(f32[6,8,16,128]{3,2,1,0:T(8,128)S(1)} %copy-done) | data formatting | bytes 786432
Async XLA Ops:
  44.7 1.7 %copy-start = (f32[6,8,16,128]{3,2,1,0:T(8,128)S(1)}, f32[6,8,16,128]{3,2,1,0:T(8,128)}, u32[]{:S(2)}) copy-start(f32[6,8,16,128]{3,2,1,0:T(8,128)} %get-tuple-element.5) | copy-start | bytes 1179652

commit v4 on v3

--- a/solution.py
+++ b/solution.py
@@ -214,7 +214,7 @@
            disp_ref, coef_ref, osem, u_ref, p_ref, f_ref, k_ref, br_ref, fl_ref, ez_ref, cz_ref, gt_ref, isem,
            e1a, e1b, s1, h1, e2a, e2b, s2, h2, rqa, rqb, e3a, s3, h3,
            u1a, u1b, carry, dga, dgb, kca, kcb, gath, rows, outb, inb,
-           send0, recv0, send1, recv1, send2, recv2, send3, recv3, asend, arecv, tsend, trecv):
+           ctake, cland, csend, crecv, send4, recv4, send0, recv0, send1, recv1, send2, recv2, send3, recv3, asend, arecv, tsend, trecv):
     X, Y = u_ref.shape[1], u_ref.shape[2]
     si, gi = lax.axis_index("slab"), lax.axis_index("grp")
     me = si * ng + gi
@@ -250,19 +250,19 @@
             ok = more if ok is None else jnp.logical_and(ok, more)
         return ok
 
-    def copies(ea, dst_a, stage, land, send, recv, low=0, high=None):
+    def copies(ea, dst_a, stage, land, send, recv, low=0, high=None, ways=8, reach=REACH):
         half = X // 2
         edge = HALO // 2
         made = []
         chans = pl.ds(low, (ea.shape[0] if high is None else high) - low)
-        for at, (ds, dg) in enumerate(steps):
+        for at, (ds, dg) in enumerate(steps[:ways]):
             if dg == 0:
                 if ds < 0:
-                    source = ea.at[chans, pl.ds(HALO, REACH)]
-                    target = dst_a.at[chans, pl.ds(HALO + X, REACH)]
+                    source = ea.at[chans, pl.ds(HALO, reach)]
+                    target = dst_a.at[chans, pl.ds(HALO + X, reach)]
                 else:
-                    source = ea.at[chans, pl.ds(HALO + X - REACH, REACH)]
-                    target = dst_a.at[chans, pl.ds(HALO - REACH, REACH)]
+                    source = ea.at[chans, pl.ds(HALO + X - reach, reach)]
+                    target = dst_a.at[chans, pl.ds(HALO - reach, reach)]
             else:
                 side = 0 if dg < 0 else 1
                 if ds == 0:
@@ -285,7 +285,7 @@
                 copy.start()
 
     def finish_recv(made, recv):
-        for at, (ds, dg) in enumerate(steps):
+        for at, (ds, dg) in enumerate(steps[:len(made)]):
             back = made[at ^ 1 if at < 4 else 11 - at][2]
 
             @pl.when(inside(ds, dg))
@@ -369,14 +369,53 @@
     blank(e2a, h2)
     blank(e3a, h3)
 
-    zeroth = copies(e1a, e1a, s1, h1, send0, recv0, 6, 7)
-    first = copies(e1a, e1a, s1, h1, send1, recv1, 0, 6)
+    def corner_copies():
+        made = []
+        for at, (ds, dg) in enumerate(steps[4:]):
+            side, end = (0 if dg < 0 else 1), (0 if ds < 0 else 1)
+            made.append((ds, dg, pltpu.make_async_remote_copy(
+                src_ref=ctake.at[side, end], dst_ref=cland.at[side, 1 - end],
+                send_sem=csend.at[at], recv_sem=crecv.at[3 - at],
+                device_id=(si + ds, gi + dg), device_id_type=MESH)))
+        return made
+
+    near = sub % 4 < 2
+    for side in range(2):
+        for end in range(2):
+            for t in range((7 + 1) // 2):
+                tile = s1[side, 2 * t, end * (X // 2 - 1)]
+                if 2 * t + 1 < 7:
+                    other = s1[side, 2 * t + 1, end * (X // 2 - 1)]
+                    tile = (jnp.where(near, tile, pltpu.roll(other, 2, 0)) if side == 0
+                            else jnp.where(near, pltpu.roll(other, 6, 0), tile))
+                ctake[side, end, t] = tile
+
+    def corner_unpack(made):
+        for at, (ds, dg) in enumerate(steps[4:]):
+            side, end = (0 if dg > 0 else 1), (1 if ds > 0 else 0)
+            pair = HALO // 2 + X // 2 if ds > 0 else HALO // 2 - 1
+            back = made[3 - at][2]
+
+            @pl.when(inside(ds, dg))
+            def _():
+                back.wait_recv()
+                for ch in range(7):
+                    tile = cland[side, end, ch // 2]
+                    h1[side, ch, pair] = tile if ch % 2 == 0 else pltpu.roll(tile, 6 if side == 0 else 2, 0)
+
+    corners = corner_copies()
+    zeroth = copies(e1a, e1a, s1, h1, send0, recv0, 6, 7, 4)
+    first = copies(e1a, e1a, s1, h1, send1, recv1, 0, 3, 4)
+    rest = copies(e1a, e1a, s1, h1, send4, recv4, 3, 6, 4, REACH - 1)
     second = copies(e2a, e2a, s2, h2, send2, recv2)
     third = copies(rqa, e3a, s3, h3, send3, recv3)
     pl.semaphore_wait(barrier, count - 1)
     begin(zeroth)
+    begin(corners)
     begin(first)
+    begin(rest)
     finish_recv(zeroth, recv0)
+    corner_unpack(corners)
 
     def open0(i, _):
         e1b[6, 2 * i], e1b[6, 2 * i + 1] = unpack(h1, 6, i)
@@ -422,6 +461,7 @@
     kcb[0, HALO - REACH] = link(e1b[6, HALO - REACH], e1b[6, HALO - REACH + 1])
     lax.fori_loop(HALO - 2, HALO + X + 2, coefficients, 0)
     finish_recv(first, recv1)
+    finish_recv(rest, recv4)
     begin(second)
     lax.fori_loop(0, (X + 2 * HALO) // 2, open1, 0)
 
@@ -575,6 +615,8 @@
         for c in range(3):
             u1a[c, x] = e1a[c, x] + (c0 * e3a[c, x] + c1 * e3a[3 + c, x])
     finish_send(zeroth)
+    finish_send(corners)
+    finish_send(rest)
     finish_send(first)
     finish_send(second)
     finish_send(third)
@@ -743,6 +785,7 @@
             ext(6), ext(6), ext(6), stage(6), land(6),
             ext(3), ext(3), vm(X, Y, Z), ext(3), ext(3), ext(5), ext(5),
             vm(2, ns * ng, 1, 128), vm(6, Y * X, Z), vm(ns, 6, zrows, 128), vm(ns, 6, zrows, 128),
+            vm(2, 2, 4, Y, Z), vm(2, 2, 4, Y, Z), dma((4,)), dma((4,)), dma((8,)), dma((8,)),
             dma((8,)), dma((8,)), dma((8,)), dma((8,)), dma((8,)), dma((8,)), dma((8,)), dma((8,)),
             dma((2,)), dma((2,)), dma((2, ns)), dma((2, ns)),
         ],

time: 47.3 us -> 46.8 us (0.989)
  Pallas kernels: 44.1 us -> 43.6 us
    pallas_call x1, Pallas kernels: 44.1 us -> 43.6 us  [fused(): pl.pallas_call(lambda *refs: kernel(ns, ng, *refs), name='lattice', out_s...]
where the time goes in v4:
time: 46.8 us; the launch traced here: 46.6 us
  Pallas kernels  43.6 us (93%)
  local copies, waits for them, and re-layouts  2.42 us (5%)
  between operations  0.65 us (1%)
    pallas_call x1, Pallas kernels, fused(): pl.pallas_call(lambda *refs: kernel(ns, ng, *refs), name='lattice', out_s...  43.6 us
    unnamed x4, local copies, waits for them, and re-layouts  2.42 us

profile of v4, /device:TPU:0, one launch (start us, length us, event | category | flops | bytes accessed | tf_op | source)
XLA Modules:
  0.0 46.6 jit_solution(4421996524834336737)
XLA Ops:
  0.6 43.6 %lattice.1 = (f32[3,16,8,128]{3,2,1,0:T(8,128)}, f32[6,8,16,128]{3,2,1,0:T(8,128)}) custom-call(f32[3,16,8,128]{3,2,1,0:T(8,128)} %refs_0_.1, f32[3,16,8,128]{3,2,1,0:T(8,128)} %refs_1_.1, f32[3,16,8,128]{3,2,1,0:T(8,128)} %refs_2_.1, f32[16,8,128]{2,1,0:T(8,128)} %refs_3_.1, s32[4,2,32]{2,1,0:T(2,128)} %refs_4_.1, s32[4,2,32]{2,1,0:T(2,128)} %refs_5_.1, ...), custom_call_target="tpu_custom_call" | custom-call | tf_op jit(solution)/shard_map/lattice/pallas_call | solution.py:771
  44.2 0.0 copy-start
  44.2 1.7 %copy.13 = f32[3,16,8,128]{3,2,1,0:T(8,128)} copy(f32[3,16,8,128]{3,2,1,0:T(8,128)} %get-tuple-element.4) | data formatting | bytes 393216
  45.9 0.0 copy-done
  45.9 0.7 %copy.14 = f32[6,8,16,128]{3,2,1,0:T(8,128)} copy(f32[6,8,16,128]{3,2,1,0:T(8,128)S(1)} %copy-done) | data formatting | bytes 786432
Async XLA Ops:
  44.2 1.7 %copy-start = (f32[6,8,16,128]{3,2,1,0:T(8,128)S(1)}, f32[6,8,16,128]{3,2,1,0:T(8,128)}, u32[]{:S(2)}) copy-start(f32[6,8,16,128]{3,2,1,0:T(8,128)} %get-tuple-element.5) | copy-start | bytes 1179652

commit v5 on v4

--- a/solution.py
+++ b/solution.py
@@ -229,12 +229,13 @@
         fetched.append(fetch)
     barrier = pltpu.get_barrier_semaphore()
 
-    def greet(i, _):
-        other = lax.rem(me + i, count)
-        pl.semaphore_signal(barrier, inc=1, device_id=(other // ng, lax.rem(other, ng)), device_id_type=MESH)
-        return 0
-
-    lax.fori_loop(1, count, greet, 0)
+    others = []
+    for k in sorted(range(ns), key=lambda k: -min(k, ns - k)):
+        for g in range(ng):
+            if k or g:
+                others.append((lax.rem(si + k, ns), lax.rem(gi + g, ng)))
+    for other in others:
+        pl.semaphore_signal(barrier, inc=1, device_id=other, device_id_type=MESH)
 
     sub, lane = sub_index(), lane_index()
     upper = sub < 4
@@ -543,14 +544,10 @@
             row = jnp.where(one == at, value, row)
         gath[step, me] = row
 
-        def share(i, _):
-            other = lax.rem(me + i, count)
+        for other in others:
             pltpu.make_async_remote_copy(
                 src_ref=gath.at[step, me], dst_ref=gath.at[step, me], send_sem=asend.at[step], recv_sem=arecv.at[step],
-                device_id=(other // ng, lax.rem(other, ng)), device_id_type=MESH).start()
-            return 0
-
-        lax.fori_loop(1, count, share, 0)
+                device_id=other, device_id_type=MESH).start()
 
     def collect(step):
         block = gath.at[step, pl.ds(0, count - 1)]
@@ -605,12 +602,13 @@
 
     lax.fori_loop(0, (X + 2 * HALO) // 2, step_b, 0)
 
-    def step_a(x, _):
-        for c in range(3):
-            u1a[c, x] = e1a[c, x] + (c0 * rqa[c, x] + c1 * rqa[3 + c, x])
-        return 0
-
-    lax.fori_loop(HALO, HALO + X, step_a, 0)
+    def step_a(i, _):
+        for x in (2 * i, 2 * i + 1):
+            for c in range(3):
+                u1a[c, x] = e1a[c, x] + (c0 * rqa[c, x] + c1 * rqa[3 + c, x])
+        return 0
+
+    lax.fori_loop(HALO // 2, (HALO + X) // 2, step_a, 0)
     for x in list(range(HALO - REACH, HALO)) + list(range(HALO + X, HALO + X + REACH)):
         for c in range(3):
             u1a[c, x] = e1a[c, x] + (c0 * e3a[c, x] + c1 * e3a[3 + c, x])

time: 46.8 us -> 45.9 us (0.981)
  Pallas kernels: 43.6 us -> 42.7 us
    pallas_call x1, Pallas kernels: 43.6 us -> 42.7 us  [fused(): pl.pallas_call(lambda *refs: kernel(ns, ng, *refs), name='lattice', out_s...]
where the time goes in v5:
time: 45.9 us; the launch traced here: 45.8 us
  Pallas kernels  42.7 us (93%)
  local copies, waits for them, and re-layouts  2.42 us (5%)
  between operations  0.65 us (1%)
    pallas_call x1, Pallas kernels, fused(): pl.pallas_call(lambda *refs: kernel(ns, ng, *refs), name='lattice', out_s...  42.7 us
    unnamed x4, local copies, waits for them, and re-layouts  2.42 us

profile of v5, /device:TPU:0, one launch (start us, length us, event | category | flops | bytes accessed | tf_op | source)
XLA Modules:
  0.0 45.8 jit_solution(3603124205972787257)
XLA Ops:
  0.6 42.7 %lattice.1 = (f32[3,16,8,128]{3,2,1,0:T(8,128)}, f32[6,8,16,128]{3,2,1,0:T(8,128)}) custom-call(f32[3,16,8,128]{3,2,1,0:T(8,128)} %refs_0_.1, f32[3,16,8,128]{3,2,1,0:T(8,128)} %refs_1_.1, f32[3,16,8,128]{3,2,1,0:T(8,128)} %refs_2_.1, f32[16,8,128]{2,1,0:T(8,128)} %refs_3_.1, s32[4,2,32]{2,1,0:T(2,128)} %refs_4_.1, s32[4,2,32]{2,1,0:T(2,128)} %refs_5_.1, ...), custom_call_target="tpu_custom_call" | custom-call | tf_op jit(solution)/shard_map/lattice/pallas_call | solution.py:769
  43.3 0.0 copy-start
  43.3 1.7 %copy.13 = f32[3,16,8,128]{3,2,1,0:T(8,128)} copy(f32[3,16,8,128]{3,2,1,0:T(8,128)} %get-tuple-element.4) | data formatting | bytes 393216
  45.0 0.0 copy-done
  45.0 0.7 %copy.14 = f32[6,8,16,128]{3,2,1,0:T(8,128)} copy(f32[6,8,16,128]{3,2,1,0:T(8,128)S(1)} %copy-done) | data formatting | bytes 786432
Async XLA Ops:
  43.3 1.7 %copy-start = (f32[6,8,16,128]{3,2,1,0:T(8,128)S(1)}, f32[6,8,16,128]{3,2,1,0:T(8,128)}, u32[]{:S(2)}) copy-start(f32[6,8,16,128]{3,2,1,0:T(8,128)} %get-tuple-element.5) | copy-start | bytes 1179652

commit v6 on v5

--- a/solution.py
+++ b/solution.py
@@ -672,7 +672,8 @@
             send_sem=tsend.at[part, i], recv_sem=trecv.at[part, i],
             device_id=(to, gi), device_id_type=MESH)
 
-    trades = [[trade(part, i) for i in range(1, ns)] for part in range(2)]
+    order = sorted(range(1, ns), key=lambda i: -min(i, ns - i))
+    trades = [[trade(part, i) for i in order] for part in range(2)]
 
     def ship(part):
         lax.fori_loop(3 * part, 3 * part + 3, transform, 0)

time: 45.9 us -> 46.2 us (level)
  no operation moved by 1% of the time
where the time goes in v6:
time: 46.2 us; the launch traced here: 46 us
  Pallas kernels  43 us (93%)
  local copies, waits for them, and re-layouts  2.42 us (5%)
  between operations  0.65 us (1%)
    pallas_call x1, Pallas kernels, fused(): pl.pallas_call(lambda *refs: kernel(ns, ng, *refs), name='lattice', out_s...  43 us
    unnamed x4, local copies, waits for them, and re-layouts  2.42 us

profile of v6, /device:TPU:0, one launch (start us, length us, event | category | flops | bytes accessed | tf_op | source)
XLA Modules:
  0.0 46.0 jit_solution(788966999343537057)
XLA Ops:
  0.6 43.0 %lattice.1 = (f32[3,16,8,128]{3,2,1,0:T(8,128)}, f32[6,8,16,128]{3,2,1,0:T(8,128)}) custom-call(f32[3,16,8,128]{3,2,1,0:T(8,128)} %refs_0_.1, f32[3,16,8,128]{3,2,1,0:T(8,128)} %refs_1_.1, f32[3,16,8,128]{3,2,1,0:T(8,128)} %refs_2_.1, f32[16,8,128]{2,1,0:T(8,128)} %refs_3_.1, s32[4,2,32]{2,1,0:T(2,128)} %refs_4_.1, s32[4,2,32]{2,1,0:T(2,128)} %refs_5_.1, ...), custom_call_target="tpu_custom_call" | custom-call | tf_op jit(solution)/shard_map/lattice/pallas_call | solution.py:770
  43.6 0.0 copy-start
  43.6 1.7 %copy.13 = f32[3,16,8,128]{3,2,1,0:T(8,128)} copy(f32[3,16,8,128]{3,2,1,0:T(8,128)} %get-tuple-element.4) | data formatting | bytes 393216
  45.3 0.0 copy-done
  45.3 0.7 %copy.14 = f32[6,8,16,128]{3,2,1,0:T(8,128)} copy(f32[6,8,16,128]{3,2,1,0:T(8,128)S(1)} %copy-done) | data formatting | bytes 786432
Async XLA Ops:
  43.6 1.7 %copy-start = (f32[6,8,16,128]{3,2,1,0:T(8,128)S(1)}, f32[6,8,16,128]{3,2,1,0:T(8,128)}, u32[]{:S(2)}) copy-start(f32[6,8,16,128]{3,2,1,0:T(8,128)} %get-tuple-element.5) | copy-start | bytes 1179652
